TPU v7x, 32 devices: a whole 2x2x4 slice. The times are simulated.
32 devices in a mesh: aux: 4 (over y, x), blk: 4 (over z), occ: 2 (over core).
Axes of the slice: x: 2, y: 2, z: 4, core: 2. Of those that a mesh axis runs over, the one named last changes fastest.
Arguments:
- integrals: bfloat16 [16, 4, 11, 512, 512], P('aux', 'blk'), may hold values from -0.078125 to 0.078125
- orbitals: bfloat16 [2048, 512], P('blk', 'occ'), may hold values from -6 to 6
- pair_lists: int32 [4, 11], P('blk'), may hold values from 0 to 3, as said below
- pair_counts: int32 [4], P('blk'), may hold values from 1 to 11, as said below
Outputs:
- exchange: float32 [4, 512, 512], P('blk', 'aux')
Inputs may be any that keep to these rules, and one draw needn't show every extreme that they name: `pair_lists`: entry 0 of row m is m itself; entries past pair_counts[m] are never read. `pair_counts`: some block has all 11 slots live.
All inputs are finite; a program needn't handle non-finite values.
Results may differ from a plain program's by a relative error of at most 0.00099.
Values may be sent and summed in bfloat16 or wider, within the bound.
No kernel may reach another device: no remote copies, remote signals or barrier semaphores. Data moves between devices by JAX's collectives and lax.ppermute only.
A program may use at most 192 MiB of HBM per device.

v0:
```python
import functools
import math

import jax
import jax.numpy as jnp
from jax import lax
from jax.experimental import pallas as pl
from jax.experimental.pallas import tpu as pltpu
from jax.sharding import PartitionSpec as P


ANY = pl.BlockSpec(memory_space=pl.ANY)
VMEM = pl.BlockSpec(memory_space=pltpu.VMEM)
SMEM = pl.BlockSpec(memory_space=pltpu.SMEM)
HBM = pl.BlockSpec(memory_space=pltpu.HBM)


def exchange_pairs(distance, size):
    return [(i, i ^ distance) for i in range(size)]


def in_hbm(x):
    return pltpu.with_memory_space_constraint(x, pltpu.HBM)


def slot_product(block_ref, coef):
    aux_total, width, _ = block_ref.shape
    flat = block_ref[...].reshape(aux_total * width, width)
    product = jnp.dot(flat, coef, preferred_element_type=jnp.float32)
    return product.reshape(aux_total, width, coef.shape[1])


def own_kernel(early, counts, lists_hbm, ints_ref, coef_hbm, acc_ref, buffer, table, coef, lists, sems, slot_sems):
    slot_total = ints_ref.shape[2]
    lists_copy = pltpu.make_async_copy(lists_hbm, lists, sems.at[0])
    lists_copy.start()
    coef_copy = pltpu.make_async_copy(coef_hbm, coef, sems.at[1])

    def fetch(i, slot):
        return pltpu.make_async_copy(ints_ref.at[:, 0, slot], buffer.at[i], slot_sems.at[i])

    fetch(0, 0).start()
    coef_copy.start()
    lists_copy.wait()
    me = lax.axis_index("blk")
    live = counts[0]
    found = jnp.int32(0)
    for step, (lo, hi) in enumerate(((0, 1), (1, 2), (2, 1 << 30))):
        for slot in range(slot_total):
            away = lists[0, slot] ^ me
            table[found] = slot
            table[slot_total + 1 + found] = away
            found = found + ((slot < live) & (away >= lo) & (away < hi)).astype(jnp.int32)
        table[2 * slot_total + 2 + step] = found
    own = jnp.minimum(table[2 * slot_total + 2], early)
    ready = jnp.minimum(live, early)

    @pl.loop(1, ready)
    def _(i):
        fetch(i, table[i]).start()

    coef_copy.wait()
    fetch(0, 0).wait()
    acc_ref[...] = slot_product(buffer.at[0], coef[...])

    @pl.loop(1, own)
    def _(i):
        fetch(i, table[i]).wait()
        acc_ref[...] += slot_product(buffer.at[i], coef[...])

    @pl.loop(own, ready)
    def _(i):
        fetch(i, table[i]).wait()


def next_kernel(early, table, ints_ref, own_hbm, next_ref, _acc, _buffer, acc_ref, buffer, coef, sems, slot_sems):
    slot_total, _, width, _ = buffer.shape
    own, near, live = (table[2 * slot_total + 2 + step] for step in range(3))

    def fetch(i):
        return pltpu.make_async_copy(ints_ref.at[:, 0, table[i]], buffer.at[i], slot_sems.at[i])

    coef_copies = [
        pltpu.make_async_copy(own_hbm, coef.at[pl.ds(0, width)], sems.at[0]),
        pltpu.make_async_copy(next_ref, coef.at[pl.ds(width, width)], sems.at[1]),
    ]
    for copy in coef_copies:
        copy.start()

    @pl.loop(early, jnp.maximum(live, early))
    def _(i):
        fetch(i).start()

    for copy in coef_copies:
        copy.wait()

    @pl.loop(jnp.minimum(own, early), near)
    def _(i):
        @pl.when(i >= early)
        def _():
            fetch(i).wait()

        rows = pl.ds(pl.multiple_of(table[slot_total + 1 + i] * width, width), width)
        acc_ref[...] += slot_product(buffer.at[i], coef[rows, :])

    @pl.loop(jnp.maximum(near, early), jnp.maximum(live, early))
    def _(i):
        fetch(i).wait()


def far_kernel(table, buffer, _acc, *rest):
    aux_size, occ_size = lax.axis_size("aux"), lax.axis_size("occ")
    chunks = rest[:aux_size]
    pieces = rest[aux_size : aux_size + occ_size]
    total, coef, halves, sems = rest[aux_size + occ_size :]
    slot_total, _, width, _ = buffer.shape
    near, live = table[2 * slot_total + 3], table[2 * slot_total + 4]
    my_aux, my_occ = lax.axis_index("aux"), lax.axis_index("occ")
    depth = chunks[0].shape[0]
    copies = []
    for k in range(aux_size):
        rows = pl.ds(pl.multiple_of((my_aux ^ k) * depth, depth), depth)
        copies.append(pltpu.make_async_copy(chunks[k], coef.at[rows], sems.at[k]))
    for copy in copies:
        copy.start()
    for copy in copies:
        copy.wait()

    @pl.loop(near, live)
    def _(i):
        rows = pl.ds(pl.multiple_of((table[slot_total + 1 + i] - 2) * width, width), width)
        total[...] += slot_product(buffer.at[i], coef[rows, :])

    columns = total.shape[2]
    for p in range(total.shape[0]):
        halves[:, p * columns : (p + 1) * columns] = total[p].astype(jnp.bfloat16)
    share = pieces[0].shape[1]
    for k in range(occ_size):
        rows = pl.ds(pl.multiple_of((my_occ ^ k) * share, share), share)
        pieces[k][...] = lax.dot_general(
            halves[...], halves[rows, :], (((1,), (1,)), ((), ())), preferred_element_type=jnp.float32
        )


def split_kernel(*refs):
    aux_size, occ_size = lax.axis_size("aux"), lax.axis_size("occ")
    terms, outs = refs[:occ_size], refs[occ_size:]
    my_aux = lax.axis_index("aux")
    depth = outs[0].shape[0]
    for k in range(aux_size):
        rows = pl.ds(pl.multiple_of((my_aux ^ k) * depth, depth), depth)
        total = terms[0][rows, :]
        for term in terms[1:]:
            total = total + term[rows, :]
        outs[k][...] = total


def per_device(integrals, orbitals, pair_lists, pair_counts):
    aux_total, _, slot_total, width, _ = integrals.shape
    columns = orbitals.shape[1]
    aux_size, blk_size, occ_size = (lax.axis_size(n) for n in ("aux", "blk", "occ"))
    my_aux, my_occ = lax.axis_index("aux"), lax.axis_index("occ")
    slot_flops = 2 * aux_total * width * width * columns
    slot_bytes = 2 * aux_total * width * width
    early = (slot_total + 1) // 2

    def cost(slots):
        return pl.CostEstimate(
            flops=slots * slot_flops, bytes_accessed=slots * slot_bytes, transcendentals=0
        )

    depth = (blk_size - 2) * width // aux_size
    piece = math.gcd(depth, width)
    parts = []
    for t in range(depth // piece):
        starts = [a * depth + t * piece for a in range(aux_size)]
        pairs = [
            (a * blk_size + i, a * blk_size + (i ^ (2 + starts[a] // width)))
            for a in range(aux_size)
            for i in range(blk_size)
        ]
        offset = (my_aux * depth + t * piece) % width
        sent = lax.dynamic_slice_in_dim(orbitals, offset, piece, 0)
        parts.append(lax.ppermute(sent, ("aux", "blk"), pairs))
    next_block = lax.ppermute(orbitals, "blk", exchange_pairs(1, blk_size))
    chunk = parts[0] if len(parts) == 1 else jnp.concatenate(parts, 0)
    chunks = [chunk] + [
        lax.ppermute(chunk, "aux", exchange_pairs(k, aux_size)) for k in range(1, aux_size)
    ]

    acc_shape = jax.ShapeDtypeStruct((aux_total, width, columns), jnp.float32)
    buffer_shape = jax.ShapeDtypeStruct((slot_total, aux_total, width, width), jnp.bfloat16)
    table_shape = jax.ShapeDtypeStruct((2 * slot_total + 5,), jnp.int32)
    slot_sems = pltpu.SemaphoreType.DMA((slot_total,))

    acc, buffer, table = pl.pallas_call(
        functools.partial(own_kernel, early),
        out_shape=(acc_shape, buffer_shape, table_shape),
        in_specs=[SMEM, HBM, HBM, HBM],
        out_specs=(VMEM, VMEM, SMEM),
        scratch_shapes=[
            pltpu.VMEM((width, columns), jnp.bfloat16),
            pltpu.SMEM(pair_lists.shape, jnp.int32),
            pltpu.SemaphoreType.DMA((2,)),
            slot_sems,
        ],
        compiler_params=pltpu.CompilerParams(vmem_limit_bytes=8 << 20),
        cost_estimate=cost(early),
        name="own",
    )(pair_counts, in_hbm(pair_lists), in_hbm(integrals), in_hbm(orbitals))
    acc, buffer = pl.pallas_call(
        functools.partial(next_kernel, early),
        out_shape=(acc_shape, buffer_shape),
        in_specs=[SMEM, HBM, HBM, ANY, VMEM, VMEM],
        out_specs=(VMEM, VMEM),
        scratch_shapes=[
            pltpu.VMEM((2 * width, columns), jnp.bfloat16),
            pltpu.SemaphoreType.DMA((2,)),
            slot_sems,
        ],
        input_output_aliases={4: 0, 5: 1},
        compiler_params=pltpu.CompilerParams(vmem_limit_bytes=8 << 20),
        cost_estimate=cost(early),
        name="next",
    )(table, in_hbm(integrals), in_hbm(orbitals), next_block, acc, buffer)

    share = width // occ_size
    *pieces, _ = pl.pallas_call(
        far_kernel,
        out_shape=[jax.ShapeDtypeStruct((width, share), jnp.float32)] * occ_size + [acc_shape],
        in_specs=[SMEM, VMEM, VMEM] + [ANY] * aux_size,
        out_specs=[VMEM] * (occ_size + 1),
        scratch_shapes=[
            pltpu.VMEM(((blk_size - 2) * width, columns), jnp.bfloat16),
            pltpu.VMEM((width, aux_total * columns), jnp.bfloat16),
            pltpu.SemaphoreType.DMA((aux_size,)),
        ],
        input_output_aliases={2: occ_size},
        compiler_params=pltpu.CompilerParams(
            vmem_limit_bytes=(6 << 20) + 2 * columns * width * (blk_size - 2)
        ),
        cost_estimate=cost(early),
        name="far",
    )(table, buffer, acc, *chunks)

    terms = [pieces[0]] + [
        lax.ppermute(pieces[k], "occ", exchange_pairs(k, occ_size)) for k in range(1, occ_size)
    ]
    rows = width // aux_size
    mine = pl.pallas_call(
        split_kernel,
        out_shape=[jax.ShapeDtypeStruct((rows, share), jnp.float32)] * aux_size,
        in_specs=[VMEM] * occ_size,
        out_specs=[VMEM] * aux_size,
        compiler_params=pltpu.CompilerParams(vmem_limit_bytes=8 << 20),
        name="split",
    )(*terms)
    total = mine[0]
    for k in range(1, aux_size):
        total = total + lax.ppermute(mine[k], "aux", exchange_pairs(k, aux_size))
    total = total / (columns * occ_size)
    shares = [total] + [
        lax.ppermute(total, "occ", exchange_pairs(k, occ_size)) for k in range(1, occ_size)
    ]
    ordered = []
    for o in range(occ_size):
        value = shares[0]
        for k in range(1, occ_size):
            value = jnp.where((my_occ ^ k) == o, shares[k], value)
        ordered.append(value)
    return jnp.concatenate(ordered, 1)[None]


def solution(mesh):
    placed = (P("aux", "blk", None, None, None), P("blk", "occ"), P("blk", None), P("blk"))
    return jax.shard_map(
        per_device, mesh=mesh, in_specs=placed, out_specs=P("blk", "aux", None), check_vma=False
    )
```

profile of v0, /device:TPU:0, one launch (start us, length us, event | category | flops | bytes accessed | tf_op | source)
XLA Modules:
  0.0 44.5 jit_solution(15822332725295045405)
XLA Ops:
  0.0 3.1 %collective-permute-start = (bf16[512,256]{1,0:T(8,128)(2,1)}, bf16[512,256]{1,0:T(8,128)(2,1)S(1)}, u32[]{:S(2)}, u32[]{:S(2)}) collective-permute-start(bf16[512,256]{1,0:T(8,128)(2,1)} %own_hbm.1), channel_id=1, source_target_pairs={{0,2},{2,0},{4,6},{6,4},{1,3},{3,1},{5,7},{7,5},{8,10},{10,8},{12,... | collective-permute-start | bytes 786440 | tf_op jit(solution)/shard_map/ppermute | solution.py:185
  3.1 0.9 %constant_dynamic-slice_fusion = bf16[256,256]{1,0:T(8,128)(2,1)S(1)} fusion(bf16[512,256]{1,0:T(8,128)(2,1)} %own_hbm.1, s32[]{:T(128)S(6)} %select_n.26), kind=kLoop, calls=%fused_computation.4 | loop fusion | bytes 262148 | tf_op jit(solution)/shard_map/dynamic_slice | solution.py:183
  4.0 2.7 %collective-permute-start.1 = (bf16[256,256]{1,0:T(8,128)(2,1)S(1)}, bf16[256,256]{1,0:T(8,128)(2,1)S(1)}, u32[]{:S(2)}, u32[]{:S(2)}) collective-permute-start(bf16[256,256]{1,0:T(8,128)(2,1)S(1)} %constant_dynamic-slice_fusion), channel_id=1, source_target_pairs={{0,4},{2,6},{4,0},{6,2},{8,12},{10,14},{12,8},{14,10},{16,22},{18,... | collective-permute-start | bytes 393224 | tf_op jit(solution)/shard_map/ppermute | solution.py:184
  7.3 5.7 %own.1 = (f32[4,512,256]{2,1,0:T(8,128)S(1)}, bf16[11,4,512,512]{3,2,1,0:T(8,128)(2,1)S(1)}, s32[27]{0:T(128)S(1)}) custom-call(s32[1]{0:T(128)S(6)} %copy.11.counts, s32[1,11]{1,0:T(1,128)} %lists_hbm.1, bf16[4,1,11,512,512]{4,3,2,1,0:T(8,128)(2,1)} %ints_ref.3, bf16[512,256]{1,0:T(8,128)(2,1)} %own_hbm.1), custom_call_target="tpu_custom_call" | custom-call | flops 3221225472 | bytes 12582912 | tf_op jit(solution)/shard_map/own/pallas_call | solution.py:196
  13.0 0.0 collective-permute-done.1.rest_0_
  13.0 1.6 %collective-permute-start.2 = (bf16[256,256]{1,0:T(8,128)(2,1)S(1)}, bf16[256,256]{1,0:T(8,128)(2,1)S(1)}, u32[]{:S(2)}, u32[]{:S(2)}) collective-permute-start(bf16[256,256]{1,0:T(8,128)(2,1)S(1)} %collective-permute-done.1.rest_0_), channel_id=1, source_target_pairs={{0,8},{8,0},{16,24},{24,16},{1,9},{9,1},{17,25},{25,17},{2,10},{10... | collective-permute-start | bytes 393224 | tf_op jit(solution)/shard_map/ppermute | solution.py:188
  14.6 3.0 %collective-permute-start.3 = (bf16[256,256]{1,0:T(8,128)(2,1)S(1)}, bf16[256,256]{1,0:T(8,128)(2,1)S(1)}, u32[]{:S(2)}, u32[]{:S(2)}) collective-permute-start(bf16[256,256]{1,0:T(8,128)(2,1)S(1)} %collective-permute-done.1.rest_0_), channel_id=1, source_target_pairs={{0,16},{8,24},{16,0},{24,8},{1,17},{9,25},{17,1},{25,9},{2,18},{10... | collective-permute-start | bytes 393224 | tf_op jit(solution)/shard_map/ppermute | solution.py:188
  17.6 0.0 collective-permute-start.4
  17.6 0.0 collective-permute-done.next_ref
  17.6 4.2 %next.1 = (f32[4,512,256]{2,1,0:T(8,128)S(1)}, bf16[11,4,512,512]{3,2,1,0:T(8,128)(2,1)S(1)}) custom-call(s32[27]{0:T(128)S(1)} %get-tuple-element.16.table, bf16[4,1,11,512,512]{4,3,2,1,0:T(8,128)(2,1)} %ints_ref.3, bf16[512,256]{1,0:T(8,128)(2,1)} %own_hbm.1, ...), custom_call_target="tpu_custom_call", output_to_operand_aliasing={{0}: (4, {}), {1}: (5, {})} | custom-call | flops 3221225472 | bytes 12582912 | tf_op jit(solution)/shard_map/next/pallas_call | solution.py:211
  21.8 0.0 collective-permute-done.2.rest_1_
  21.8 0.2 collective-permute-done.3.rest_2_
  22.0 1.4 %collective-permute-done.4.rest_3_ = bf16[256,256]{1,0:T(8,128)(2,1)S(1)} collective-permute-done((bf16[256,256]{1,0:T(8,128)(2,1)S(1)}, bf16[256,256]{1,0:T(8,128)(2,1)S(1)}, u32[]{:S(2)}, u32[]{:S(2)}) %collective-permute-start.4) | collective-permute-done | bytes 131104 | tf_op jit(solution)/shard_map/ppermute | solution.py:188
  23.4 7.5 %far.1 = (f32[512,256]{1,0:T(8,128)S(1)}, f32[512,256]{1,0:T(8,128)S(1)}, f32[4,512,256]{2,1,0:T(8,128)S(1)}) custom-call(s32[27]{0:T(128)S(1)} %get-tuple-element.16.table, bf16[11,4,512,512]{3,2,1,0:T(8,128)(2,1)S(1)} %get-tuple-element.19.buffer, f32[4,512,256]{2,1,0:T(8,128)S(1)} %get-tuple-element.20._acc, ...), custom_call_target="tpu_custom_call", output_to_operand_aliasing={{2}: (2, {})} | custom-call | flops 3221225472 | bytes 12582912 | tf_op jit(solution)/shard_map/far/pallas_call | solution.py:228
  30.9 0.1 collective-permute-start.5
  31.0 1.9 %collective-permute-done.5.refs_1_ = f32[512,256]{1,0:T(8,128)S(1)} collective-permute-done((f32[512,256]{1,0:T(8,128)S(1)}, f32[512,256]{1,0:T(8,128)S(1)}, u32[]{:S(2)}, u32[]{:S(2)}) %collective-permute-start.5) | collective-permute-done | bytes 524320 | tf_op jit(solution)/shard_map/ppermute | solution.py:247
  32.9 0.1 split.1
  32.9 1.4 %collective-permute-start.8 = (f32[128,256]{1,0:T(8,128)S(1)}, f32[128,256]{1,0:T(8,128)S(1)}, u32[]{:S(2)}, u32[]{:S(2)}) collective-permute-start(f32[128,256]{1,0:T(8,128)S(1)} %get-tuple-element.26), channel_id=1, source_target_pairs={{0,24},{8,16},{16,8},{24,0},{1,25},{9,17},{17,9},{25,1},{2,26},{10... | collective-permute-start | bytes 393224 | tf_op jit(solution)/shard_map/ppermute | solution.py:260
  34.3 0.9 %collective-permute-start.7 = (f32[128,256]{1,0:T(8,128)S(1)}, f32[128,256]{1,0:T(8,128)S(1)}, u32[]{:S(2)}, u32[]{:S(2)}) collective-permute-start(f32[128,256]{1,0:T(8,128)S(1)} %get-tuple-element.25), channel_id=1, source_target_pairs={{0,16},{8,24},{16,0},{24,8},{1,17},{9,25},{17,1},{25,9},{2,18},{10... | collective-permute-start | bytes 393224 | tf_op jit(solution)/shard_map/ppermute | solution.py:260
  35.3 1.2 %collective-permute-start.6 = (f32[128,256]{1,0:T(8,128)S(1)}, f32[128,256]{1,0:T(8,128)S(1)}, u32[]{:S(2)}, u32[]{:S(2)}) collective-permute-start(f32[128,256]{1,0:T(8,128)S(1)} %get-tuple-element.24), channel_id=1, source_target_pairs={{0,8},{8,0},{16,24},{24,16},{1,9},{9,1},{17,25},{25,17},{2,10},{10... | collective-permute-start | bytes 393224 | tf_op jit(solution)/shard_map/ppermute | solution.py:260
  36.5 3.8 %collective-permute-done.8 = f32[128,256]{1,0:T(8,128)S(1)} collective-permute-done((f32[128,256]{1,0:T(8,128)S(1)}, f32[128,256]{1,0:T(8,128)S(1)}, u32[]{:S(2)}, u32[]{:S(2)}) %collective-permute-start.8) | collective-permute-done | bytes 131104 | tf_op jit(solution)/shard_map/ppermute | solution.py:260
  40.3 1.9 %collective-permute-done.7 = f32[128,256]{1,0:T(8,128)S(1)} collective-permute-done((f32[128,256]{1,0:T(8,128)S(1)}, f32[128,256]{1,0:T(8,128)S(1)}, u32[]{:S(2)}, u32[]{:S(2)}) %collective-permute-start.7) | collective-permute-done | bytes 131104 | tf_op jit(solution)/shard_map/ppermute | solution.py:260
  42.3 0.0 collective-permute-done.6
  42.3 0.1 collective-permute-start.9
  42.4 1.3 %collective-permute-done.9 = f32[128,256]{1,0:T(8,128)S(1)} collective-permute-done((f32[128,256]{1,0:T(8,128)S(1)}, f32[128,256]{1,0:T(8,128)S(1)}, u32[]{:S(2)}, u32[]{:S(2)}) %collective-permute-start.9) | collective-permute-done | bytes 131104 | tf_op jit(solution)/shard_map/ppermute | solution.py:263
  43.7 0.7 %maximum_bitcast_fusion = f32[1,128,512]{2,1,0:T(8,128)} fusion(f32[128,256]{1,0:T(8,128)S(1)} %get-tuple-element.28, f32[128,256]{1,0:T(8,128)S(1)} %get-tuple-element.27), kind=kLoop, calls=%fused_computation | loop fusion | flops 65536 | bytes 524288 | tf_op jit(solution)/shard_map/broadcast_in_dim | solution.py:271
  (2 shorter events, 0.1 us)
Async XLA Ops:
  0.0 17.6 %collective-permute-start = (bf16[512,256]{1,0:T(8,128)(2,1)}, bf16[512,256]{1,0:T(8,128)(2,1)S(1)}, u32[]{:S(2)}, u32[]{:S(2)}) collective-permute-start(bf16[512,256]{1,0:T(8,128)(2,1)} %own_hbm.1), channel_id=1, source_target_pairs={{0,2},{2,0},{4,6},{6,4},{1,3},{3,1},{5,7},{7,5},{8,10},{10,8},{12,... | collective-permute-start | bytes 786440 | tf_op jit(solution)/shard_map/ppermute | solution.py:185
  4.0 9.0 %collective-permute-start.1 = (bf16[256,256]{1,0:T(8,128)(2,1)S(1)}, bf16[256,256]{1,0:T(8,128)(2,1)S(1)}, u32[]{:S(2)}, u32[]{:S(2)}) collective-permute-start(bf16[256,256]{1,0:T(8,128)(2,1)S(1)} %constant_dynamic-slice_fusion), channel_id=1, source_target_pairs={{0,4},{2,6},{4,0},{6,2},{8,12},{10,14},{12,8},{14,10},{16,22},{18,... | collective-permute-start | bytes 393224 | tf_op jit(solution)/shard_map/ppermute | solution.py:184
  13.0 8.8 %collective-permute-start.2 = (bf16[256,256]{1,0:T(8,128)(2,1)S(1)}, bf16[256,256]{1,0:T(8,128)(2,1)S(1)}, u32[]{:S(2)}, u32[]{:S(2)}) collective-permute-start(bf16[256,256]{1,0:T(8,128)(2,1)S(1)} %collective-permute-done.1.rest_0_), channel_id=1, source_target_pairs={{0,8},{8,0},{16,24},{24,16},{1,9},{9,1},{17,25},{25,17},{2,10},{10... | collective-permute-start | bytes 393224 | tf_op jit(solution)/shard_map/ppermute | solution.py:188
  14.6 7.4 %collective-permute-start.3 = (bf16[256,256]{1,0:T(8,128)(2,1)S(1)}, bf16[256,256]{1,0:T(8,128)(2,1)S(1)}, u32[]{:S(2)}, u32[]{:S(2)}) collective-permute-start(bf16[256,256]{1,0:T(8,128)(2,1)S(1)} %collective-permute-done.1.rest_0_), channel_id=1, source_target_pairs={{0,16},{8,24},{16,0},{24,8},{1,17},{9,25},{17,1},{25,9},{2,18},{10... | collective-permute-start | bytes 393224 | tf_op jit(solution)/shard_map/ppermute | solution.py:188
  17.6 5.9 %collective-permute-start.4 = (bf16[256,256]{1,0:T(8,128)(2,1)S(1)}, bf16[256,256]{1,0:T(8,128)(2,1)S(1)}, u32[]{:S(2)}, u32[]{:S(2)}) collective-permute-start(bf16[256,256]{1,0:T(8,128)(2,1)S(1)} %collective-permute-done.1.rest_0_), channel_id=1, source_target_pairs={{0,24},{8,16},{16,8},{24,0},{1,25},{9,17},{17,9},{25,1},{2,26},{10... | collective-permute-start | bytes 393224 | tf_op jit(solution)/shard_map/ppermute | solution.py:188
  30.9 2.0 %collective-permute-start.5 = (f32[512,256]{1,0:T(8,128)S(1)}, f32[512,256]{1,0:T(8,128)S(1)}, u32[]{:S(2)}, u32[]{:S(2)}) collective-permute-start(f32[512,256]{1,0:T(8,128)S(1)} %get-tuple-element.22), channel_id=1, source_target_pairs={{0,1},{1,0},{2,3},{3,2},{4,5},{5,4},{6,7},{7,6},{8,9},{9,8},{10,11... | collective-permute-start | bytes 1572872 | tf_op jit(solution)/shard_map/ppermute | solution.py:247
  32.9 7.4 %collective-permute-start.8 = (f32[128,256]{1,0:T(8,128)S(1)}, f32[128,256]{1,0:T(8,128)S(1)}, u32[]{:S(2)}, u32[]{:S(2)}) collective-permute-start(f32[128,256]{1,0:T(8,128)S(1)} %get-tuple-element.26), channel_id=1, source_target_pairs={{0,24},{8,16},{16,8},{24,0},{1,25},{9,17},{17,9},{25,1},{2,26},{10... | collective-permute-start | bytes 393224 | tf_op jit(solution)/shard_map/ppermute | solution.py:260
  34.3 7.9 %collective-permute-start.7 = (f32[128,256]{1,0:T(8,128)S(1)}, f32[128,256]{1,0:T(8,128)S(1)}, u32[]{:S(2)}, u32[]{:S(2)}) collective-permute-start(f32[128,256]{1,0:T(8,128)S(1)} %get-tuple-element.25), channel_id=1, source_target_pairs={{0,16},{8,24},{16,0},{24,8},{1,17},{9,25},{17,1},{25,9},{2,18},{10... | collective-permute-start | bytes 393224 | tf_op jit(solution)/shard_map/ppermute | solution.py:260
  35.3 7.0 %collective-permute-start.6 = (f32[128,256]{1,0:T(8,128)S(1)}, f32[128,256]{1,0:T(8,128)S(1)}, u32[]{:S(2)}, u32[]{:S(2)}) collective-permute-start(f32[128,256]{1,0:T(8,128)S(1)} %get-tuple-element.24), channel_id=1, source_target_pairs={{0,8},{8,0},{16,24},{24,16},{1,9},{9,1},{17,25},{25,17},{2,10},{10... | collective-permute-start | bytes 393224 | tf_op jit(solution)/shard_map/ppermute | solution.py:260
  42.3 1.4 %collective-permute-start.9 = (f32[128,256]{1,0:T(8,128)S(1)}, f32[128,256]{1,0:T(8,128)S(1)}, u32[]{:S(2)}, u32[]{:S(2)}) collective-permute-start(f32[128,256]{1,0:T(8,128)S(1)} %add_multiply_fusion), channel_id=1, source_target_pairs={{0,1},{1,0},{2,3},{3,2},{4,5},{5,4},{6,7},{7,6},{8,9},{9,8},{10,11... | collective-permute-start | bytes 393224 | tf_op jit(solution)/shard_map/ppermute | solution.py:263
where the time goes:
time: 44.6 us; the launch traced here: 44.5 us
  Pallas kernels  17.4 us (39%)
  starting transfers between devices  14 us (31%)
  waiting for transfers between devices  10.6 us (24%)
  local copies, waits for them, and re-layouts  0.95 us (2%)
  other arithmetic  0.78 us (2%)
  between operations  0.73 us (2%)
    pallas_call x1, Pallas kernels, per_device(): pl.pallas_call(far_kernel, out_shape=[jax.ShapeDtypeStruct((width, share)...  7.45 us
    ppermute x3, waiting for transfers between devices, per_device(): total = total + lax.ppermute(mine[k], 'aux', exchange_pairs(k, aux_size))  5.76 us
    pallas_call x1, Pallas kernels, per_device(): pl.pallas_call(functools.partial(own_kernel, early), out_shape=(acc_shape...  5.7 us
    ppermute x3, starting transfers between devices, per_device(): lax.ppermute(chunk, 'aux', exchange_pairs(k, aux_size))  4.55 us
    pallas_call x1, Pallas kernels, per_device(): pl.pallas_call(functools.partial(next_kernel, early), out_shape=(acc_shap...  4.21 us
    ppermute x3, starting transfers between devices, per_device(): total = total + lax.ppermute(mine[k], 'aux', exchange_pairs(k, aux_size))  3.55 us
    ppermute x1, starting transfers between devices, per_device(): next_block = lax.ppermute(orbitals, 'blk', exchange_pairs(1, blk_size))  3.05 us
    ppermute x1, starting transfers between devices, per_device(): parts.append(lax.ppermute(sent, ('aux', 'blk'), pairs))  2.65 us
  transfers between devices with their start and end apart: 10, of which 6 were waited for; matrix products, arithmetic and copies ran while one was open for 2% of the time, Pallas kernels for 22%

commit v1 on v0

--- a/solution.py
+++ b/solution.py
@@ -28,6 +28,24 @@
     flat = block_ref[...].reshape(aux_total * width, width)
     product = jnp.dot(flat, coef, preferred_element_type=jnp.float32)
     return product.reshape(aux_total, width, coef.shape[1])
+
+
+def add_far(table, i, distance, buffer, chunk_ref, acc_ref):
+    slot_total, aux_total, width, _ = buffer.shape
+    depth, columns = chunk_ref.shape
+    piece = math.gcd(depth, width)
+    base = (lax.axis_index("aux") ^ distance) * depth
+    for part in range(width // piece):
+        local = (table[slot_total + 1 + i] - 2) * width + part * piece - base
+
+        @pl.when((local >= 0) & (local < depth))
+        def _():
+            left = buffer[i, :, :, part * piece : (part + 1) * piece]
+            right = chunk_ref[pl.ds(pl.multiple_of(local, piece), piece), :]
+            product = jnp.dot(
+                left.reshape(aux_total * width, piece), right, preferred_element_type=jnp.float32
+            )
+            acc_ref[...] += product.reshape(aux_total, width, columns)
 
 
 def own_kernel(early, counts, lists_hbm, ints_ref, coef_hbm, acc_ref, buffer, table, coef, lists, sems, slot_sems):
@@ -73,7 +91,7 @@
         fetch(i, table[i]).wait()
 
 
-def next_kernel(early, table, ints_ref, own_hbm, next_ref, _acc, _buffer, acc_ref, buffer, coef, sems, slot_sems):
+def next_kernel(early, table, ints_ref, own_hbm, next_ref, chunk_ref, _acc, _buffer, acc_ref, buffer, coef, sems, slot_sems):
     slot_total, _, width, _ = buffer.shape
     own, near, live = (table[2 * slot_total + 2 + step] for step in range(3))
 
@@ -103,43 +121,39 @@
         rows = pl.ds(pl.multiple_of(table[slot_total + 1 + i] * width, width), width)
         acc_ref[...] += slot_product(buffer.at[i], coef[rows, :])
 
-    @pl.loop(jnp.maximum(near, early), jnp.maximum(live, early))
-    def _(i):
-        fetch(i).wait()
-
-
-def far_kernel(table, buffer, _acc, *rest):
-    aux_size, occ_size = lax.axis_size("aux"), lax.axis_size("occ")
-    chunks = rest[:aux_size]
-    pieces = rest[aux_size : aux_size + occ_size]
-    total, coef, halves, sems = rest[aux_size + occ_size :]
-    slot_total, _, width, _ = buffer.shape
-    near, live = table[2 * slot_total + 3], table[2 * slot_total + 4]
-    my_aux, my_occ = lax.axis_index("aux"), lax.axis_index("occ")
-    depth = chunks[0].shape[0]
-    copies = []
-    for k in range(aux_size):
-        rows = pl.ds(pl.multiple_of((my_aux ^ k) * depth, depth), depth)
-        copies.append(pltpu.make_async_copy(chunks[k], coef.at[rows], sems.at[k]))
-    for copy in copies:
-        copy.start()
-    for copy in copies:
-        copy.wait()
-
     @pl.loop(near, live)
     def _(i):
-        rows = pl.ds(pl.multiple_of((table[slot_total + 1 + i] - 2) * width, width), width)
-        total[...] += slot_product(buffer.at[i], coef[rows, :])
-
-    columns = total.shape[2]
-    for p in range(total.shape[0]):
-        halves[:, p * columns : (p + 1) * columns] = total[p].astype(jnp.bfloat16)
-    share = pieces[0].shape[1]
-    for k in range(occ_size):
-        rows = pl.ds(pl.multiple_of((my_occ ^ k) * share, share), share)
-        pieces[k][...] = lax.dot_general(
-            halves[...], halves[rows, :], (((1,), (1,)), ((), ())), preferred_element_type=jnp.float32
-        )
+        @pl.when(i >= early)
+        def _():
+            fetch(i).wait()
+
+        add_far(table, i, 0, buffer, chunk_ref, acc_ref)
+
+
+def far_kernel(distance, table, buffer, chunk_ref, _acc, acc_ref):
+    slot_total = buffer.shape[0]
+
+    @pl.loop(table[2 * slot_total + 3], table[2 * slot_total + 4])
+    def _(i):
+        add_far(table, i, distance, buffer, chunk_ref, acc_ref)
+
+
+def last_kernel(distance, table, buffer, chunk_ref, _acc, acc_ref, halves, *pieces):
+    far_kernel(distance, table, buffer, chunk_ref, _acc, acc_ref)
+    columns = acc_ref.shape[2]
+    for p in range(acc_ref.shape[0]):
+        halves[:, p * columns : (p + 1) * columns] = acc_ref[p].astype(jnp.bfloat16)
+    for k, piece_ref in enumerate(pieces, 1):
+        share_kernel(k, halves, piece_ref)
+
+
+def share_kernel(distance, halves, piece_ref):
+    share = piece_ref.shape[1]
+    start = (lax.axis_index("occ") ^ distance) * share
+    rows = pl.ds(pl.multiple_of(start, share), share)
+    piece_ref[...] = lax.dot_general(
+        halves[...], halves[rows, :], (((1,), (1,)), ((), ())), preferred_element_type=jnp.float32
+    )
 
 
 def split_kernel(*refs):
@@ -162,7 +176,7 @@
     my_aux, my_occ = lax.axis_index("aux"), lax.axis_index("occ")
     slot_flops = 2 * aux_total * width * width * columns
     slot_bytes = 2 * aux_total * width * width
-    early = (slot_total + 1) // 2
+    early = (slot_total + 2) // 4
 
     def cost(slots):
         return pl.CostEstimate(
@@ -211,40 +225,55 @@
     acc, buffer = pl.pallas_call(
         functools.partial(next_kernel, early),
         out_shape=(acc_shape, buffer_shape),
-        in_specs=[SMEM, HBM, HBM, ANY, VMEM, VMEM],
+        in_specs=[SMEM, HBM, HBM, ANY, VMEM, VMEM, VMEM],
         out_specs=(VMEM, VMEM),
         scratch_shapes=[
             pltpu.VMEM((2 * width, columns), jnp.bfloat16),
             pltpu.SemaphoreType.DMA((2,)),
             slot_sems,
         ],
-        input_output_aliases={4: 0, 5: 1},
+        input_output_aliases={5: 0, 6: 1},
         compiler_params=pltpu.CompilerParams(vmem_limit_bytes=8 << 20),
         cost_estimate=cost(early),
         name="next",
-    )(table, in_hbm(integrals), in_hbm(orbitals), next_block, acc, buffer)
+    )(table, in_hbm(integrals), in_hbm(orbitals), next_block, chunk, acc, buffer)
 
     share = width // occ_size
-    *pieces, _ = pl.pallas_call(
-        far_kernel,
-        out_shape=[jax.ShapeDtypeStruct((width, share), jnp.float32)] * occ_size + [acc_shape],
-        in_specs=[SMEM, VMEM, VMEM] + [ANY] * aux_size,
+    piece_shape = jax.ShapeDtypeStruct((width, share), jnp.float32)
+    halves_shape = jax.ShapeDtypeStruct((width, aux_total * columns), jnp.bfloat16)
+    small = pltpu.CompilerParams(vmem_limit_bytes=8 << 20)
+    for k in range(1, aux_size - 1):
+        acc = pl.pallas_call(
+            functools.partial(far_kernel, k),
+            out_shape=acc_shape,
+            in_specs=[SMEM, VMEM, VMEM, VMEM],
+            out_specs=VMEM,
+            input_output_aliases={3: 0},
+            compiler_params=small,
+            cost_estimate=cost(1),
+        )(table, buffer, chunks[k], acc)
+    _, halves, *pieces = pl.pallas_call(
+        functools.partial(last_kernel, aux_size - 1),
+        out_shape=[acc_shape, halves_shape] + [piece_shape] * (occ_size - 1),
+        in_specs=[SMEM, VMEM, VMEM, VMEM],
         out_specs=[VMEM] * (occ_size + 1),
-        scratch_shapes=[
-            pltpu.VMEM(((blk_size - 2) * width, columns), jnp.bfloat16),
-            pltpu.VMEM((width, aux_total * columns), jnp.bfloat16),
-            pltpu.SemaphoreType.DMA((aux_size,)),
-        ],
-        input_output_aliases={2: occ_size},
-        compiler_params=pltpu.CompilerParams(
-            vmem_limit_bytes=(6 << 20) + 2 * columns * width * (blk_size - 2)
-        ),
-        cost_estimate=cost(early),
-        name="far",
-    )(table, buffer, acc, *chunks)
-
-    terms = [pieces[0]] + [
-        lax.ppermute(pieces[k], "occ", exchange_pairs(k, occ_size)) for k in range(1, occ_size)
+        input_output_aliases={3: 0},
+        compiler_params=small,
+        cost_estimate=cost(1),
+        name="last",
+    )(table, buffer, chunks[aux_size - 1], acc)
+    kept = pl.pallas_call(
+        functools.partial(share_kernel, 0),
+        out_shape=piece_shape,
+        in_specs=[VMEM],
+        out_specs=VMEM,
+        compiler_params=small,
+        cost_estimate=cost(1),
+        name="kept",
+    )(halves)
+
+    terms = [kept] + [
+        lax.ppermute(pieces[k - 1], "occ", exchange_pairs(k, occ_size)) for k in range(1, occ_size)
     ]
     rows = width // aux_size
     mine = pl.pallas_call(

time: 44.6 us -> 46.2 us (1.036)
  Pallas kernels: 17.4 us -> 19 us
  waiting for transfers between devices: 10.6 us -> 9.12 us
  starting transfers between devices: 14 us -> 15.3 us
    pallas_call x1, Pallas kernels: 4.21 us -> 6 us  [per_device(): pl.pallas_call(functools.partial(next_kernel, early), out_shape=(acc_shap...]
    pallas_call x1, Pallas kernels: 5.7 us -> 4.03 us  [per_device(): pl.pallas_call(functools.partial(own_kernel, early), out_shape=(acc_shape...]
    ppermute x3, waiting for transfers between devices: 1.64 us -> 0.01 us  [per_device(): lax.ppermute(chunk, 'aux', exchange_pairs(k, aux_size))]
    pallas_call x1 -> x4, Pallas kernels: 7.45 us -> 8.95 us  [the longest x2 4.84 us: per_device(): pl.pallas_call(functools.partial(far_kernel, k), out_shape=acc_shape, in_...]
    ppermute x3, starting transfers between devices: 4.55 us -> 5.94 us  [per_device(): lax.ppermute(chunk, 'aux', exchange_pairs(k, aux_size))]
    ppermute x1, waiting for transfers between devices: 1.9 us -> 1.41 us  [per_device(): lax.ppermute(pieces[k - 1], 'occ', exchange_pairs(k, occ_size))]
  transfers between devices with their start and end apart: 10 -> 10, of which waited for: 6 -> 5; matrix products, arithmetic and copies ran while one was open for 2% -> 2% of each run, Pallas kernels for 22% -> 33%
where the time goes in v1:
time: 46.2 us; the launch traced here: 46 us
  Pallas kernels  19 us (41%)
  starting transfers between devices  15.3 us (33%)
  waiting for transfers between devices  9.12 us (20%)
  local copies, waits for them, and re-layouts  0.95 us (2%)
  other arithmetic  0.78 us (2%)
  between operations  0.77 us (2%)
    ppermute x3, waiting for transfers between devices, per_device(): total = total + lax.ppermute(mine[k], 'aux', exchange_pairs(k, aux_size))  6.08 us
    pallas_call x1, Pallas kernels, per_device(): pl.pallas_call(functools.partial(next_kernel, early), out_shape=(acc_shap...  6 us
    ppermute x3, starting transfers between devices, per_device(): lax.ppermute(chunk, 'aux', exchange_pairs(k, aux_size))  5.94 us
    pallas_call x2, Pallas kernels, per_device(): pl.pallas_call(functools.partial(far_kernel, k), out_shape=acc_shape, in_...  4.84 us
    pallas_call x1, Pallas kernels, per_device(): pl.pallas_call(functools.partial(own_kernel, early), out_shape=(acc_shape...  4.03 us
    pallas_call x1, Pallas kernels, per_device(): pl.pallas_call(functools.partial(last_kernel, aux_size - 1), out_shape=[a...  3.64 us
    ppermute x3, starting transfers between devices, per_device(): total = total + lax.ppermute(mine[k], 'aux', exchange_pairs(k, aux_size))  3.55 us
    ppermute x1, starting transfers between devices, per_device(): next_block = lax.ppermute(orbitals, 'blk', exchange_pairs(1, blk_size))  3.05 us
  transfers between devices with their start and end apart: 10, of which 5 were waited for; matrix products, arithmetic and copies ran while one was open for 2% of the time, Pallas kernels for 33%

profile of v1, /device:TPU:0, one launch (start us, length us, event | category | flops | bytes accessed | tf_op | source)
XLA Modules:
  0.0 46.0 jit_solution(10965735445984214291)
XLA Ops:
  0.0 3.1 %collective-permute-start = (bf16[512,256]{1,0:T(8,128)(2,1)}, bf16[512,256]{1,0:T(8,128)(2,1)S(1)}, u32[]{:S(2)}, u32[]{:S(2)}) collective-permute-start(bf16[512,256]{1,0:T(8,128)(2,1)} %own_hbm.1), channel_id=1, source_target_pairs={{0,2},{2,0},{4,6},{6,4},{1,3},{3,1},{5,7},{7,5},{8,10},{10,8},{12,... | collective-permute-start | bytes 786440 | tf_op jit(solution)/shard_map/ppermute | solution.py:199
  3.1 0.9 %constant_dynamic-slice_fusion = bf16[256,256]{1,0:T(8,128)(2,1)S(1)} fusion(bf16[512,256]{1,0:T(8,128)(2,1)} %own_hbm.1, s32[]{:T(128)S(6)} %select_n.26), kind=kLoop, calls=%fused_computation.4 | loop fusion | bytes 262148 | tf_op jit(solution)/shard_map/dynamic_slice | solution.py:197
  4.0 2.7 %collective-permute-start.1 = (bf16[256,256]{1,0:T(8,128)(2,1)S(1)}, bf16[256,256]{1,0:T(8,128)(2,1)S(1)}, u32[]{:S(2)}, u32[]{:S(2)}) collective-permute-start(bf16[256,256]{1,0:T(8,128)(2,1)S(1)} %constant_dynamic-slice_fusion), channel_id=1, source_target_pairs={{0,4},{2,6},{4,0},{6,2},{8,12},{10,14},{12,8},{14,10},{16,22},{18,... | collective-permute-start | bytes 393224 | tf_op jit(solution)/shard_map/ppermute | solution.py:198
  7.3 4.0 %own.1 = (f32[4,512,256]{2,1,0:T(8,128)S(1)}, bf16[11,4,512,512]{3,2,1,0:T(8,128)(2,1)S(1)}, s32[27]{0:T(128)S(1)}) custom-call(s32[1]{0:T(128)S(6)} %copy.15.counts, s32[1,11]{1,0:T(1,128)} %lists_hbm.1, bf16[4,1,11,512,512]{4,3,2,1,0:T(8,128)(2,1)} %ints_ref.3, bf16[512,256]{1,0:T(8,128)(2,1)} %own_hbm.1), custom_call_target="tpu_custom_call" | custom-call | flops 1610612736 | bytes 6291456 | tf_op jit(solution)/shard_map/own/pallas_call | solution.py:210
  11.3 0.3 collective-permute-done.1.chunk_ref
  11.6 1.5 %collective-permute-start.4 = (bf16[256,256]{1,0:T(8,128)(2,1)S(1)}, bf16[256,256]{1,0:T(8,128)(2,1)S(1)}, u32[]{:S(2)}, u32[]{:S(2)}) collective-permute-start(bf16[256,256]{1,0:T(8,128)(2,1)S(1)} %collective-permute-done.1.chunk_ref), channel_id=1, source_target_pairs={{0,8},{8,0},{16,24},{24,16},{1,9},{9,1},{17,25},{25,17},{2,10},{10... | collective-permute-start | bytes 393224 | tf_op jit(solution)/shard_map/ppermute | solution.py:202
  13.1 4.4 %collective-permute-start.3 = (bf16[256,256]{1,0:T(8,128)(2,1)S(1)}, bf16[256,256]{1,0:T(8,128)(2,1)S(1)}, u32[]{:S(2)}, u32[]{:S(2)}) collective-permute-start(bf16[256,256]{1,0:T(8,128)(2,1)S(1)} %collective-permute-done.1.chunk_ref), channel_id=1, source_target_pairs={{0,16},{8,24},{16,0},{24,8},{1,17},{9,25},{17,1},{25,9},{2,18},{10... | collective-permute-start | bytes 393224 | tf_op jit(solution)/shard_map/ppermute | solution.py:202
  17.6 0.0 collective-permute-start.2
  17.6 0.0 collective-permute-done.next_ref
  17.6 6.0 %next.1 = (f32[4,512,256]{2,1,0:T(8,128)S(1)}, bf16[11,4,512,512]{3,2,1,0:T(8,128)(2,1)S(1)}) custom-call(s32[27]{0:T(128)S(1)} %get-tuple-element.16.table, bf16[4,1,11,512,512]{4,3,2,1,0:T(8,128)(2,1)} %ints_ref.3, bf16[512,256]{1,0:T(8,128)(2,1)} %own_hbm.1, ...), custom_call_target="tpu_custom_call", output_to_operand_aliasing={{0}: (5, {}), {1}: (6, {})} | custom-call | flops 1610612736 | bytes 6291456 | tf_op jit(solution)/shard_map/next/pallas_call | solution.py:225
  23.6 0.0 collective-permute-done.4.chunk_ref
  23.6 1.7 %shard_map.46._acc = f32[4,512,256]{2,1,0:T(8,128)S(1)} custom-call(s32[27]{0:T(128)S(1)} %get-tuple-element.16.table, bf16[11,4,512,512]{3,2,1,0:T(8,128)(2,1)S(1)} %get-tuple-element.19.buffer, bf16[256,256]{1,0:T(8,128)(2,1)S(1)} %collective-permute-done.4.chunk_ref, f32[4,512,256]{2,1,0:T(8,128)S(1)} %get-tuple-element.20._acc), custom_call_target="tpu_custom_call", output_to_operand_aliasing={{}: (3, {})} | custom-call | flops 536870912 | bytes 2097152 | tf_op jit(solution)/shard_map/pallas_call | solution.py:246
  25.3 0.0 collective-permute-done.3.chunk_ref
  25.3 3.2 %shard_map.47._acc = f32[4,512,256]{2,1,0:T(8,128)S(1)} custom-call(s32[27]{0:T(128)S(1)} %get-tuple-element.16.table, bf16[11,4,512,512]{3,2,1,0:T(8,128)(2,1)S(1)} %get-tuple-element.19.buffer, bf16[256,256]{1,0:T(8,128)(2,1)S(1)} %collective-permute-done.3.chunk_ref, f32[4,512,256]{2,1,0:T(8,128)S(1)} %shard_map.46._acc), custom_call_target="tpu_custom_call", output_to_operand_aliasing={{}: (3, {})} | custom-call | flops 536870912 | bytes 2097152 | tf_op jit(solution)/shard_map/pallas_call | solution.py:246
  28.5 0.0 collective-permute-done.2.chunk_ref
  28.5 3.6 %last.1 = (f32[4,512,256]{2,1,0:T(8,128)S(1)}, bf16[512,1024]{1,0:T(8,128)(2,1)S(1)}, f32[512,256]{1,0:T(8,128)S(1)}) custom-call(s32[27]{0:T(128)S(1)} %get-tuple-element.16.table, bf16[11,4,512,512]{3,2,1,0:T(8,128)(2,1)S(1)} %get-tuple-element.19.buffer, bf16[256,256]{1,0:T(8,128)(2,1)S(1)} %collective-permute-done.2.chunk_ref, ...), custom_call_target="tpu_custom_call", output_to_operand_aliasing={{0}: (3, {})} | custom-call | flops 536870912 | bytes 2097152 | tf_op jit(solution)/shard_map/last/pallas_call | solution.py:255
  32.1 0.1 collective-permute-start.5
  32.2 0.5 %kept.1.refs_0_ = f32[512,256]{1,0:T(8,128)S(1)} custom-call(bf16[512,1024]{1,0:T(8,128)(2,1)S(1)} %get-tuple-element.21.halves), custom_call_target="tpu_custom_call" | custom-call | flops 536870912 | bytes 2097152 | tf_op jit(solution)/shard_map/kept/pallas_call | solution.py:265
  32.7 1.4 %collective-permute-done.5.refs_1_ = f32[512,256]{1,0:T(8,128)S(1)} collective-permute-done((f32[512,256]{1,0:T(8,128)S(1)}, f32[512,256]{1,0:T(8,128)S(1)}, u32[]{:S(2)}, u32[]{:S(2)}) %collective-permute-start.5) | collective-permute-done | bytes 524320 | tf_op jit(solution)/shard_map/ppermute | solution.py:276
  34.1 0.1 split.1
  34.2 1.6 %collective-permute-start.6 = (f32[128,256]{1,0:T(8,128)S(1)}, f32[128,256]{1,0:T(8,128)S(1)}, u32[]{:S(2)}, u32[]{:S(2)}) collective-permute-start(f32[128,256]{1,0:T(8,128)S(1)} %get-tuple-element.24), channel_id=1, source_target_pairs={{0,8},{8,0},{16,24},{24,16},{1,9},{9,1},{17,25},{25,17},{2,10},{10... | collective-permute-start | bytes 393224 | tf_op jit(solution)/shard_map/ppermute | solution.py:289
  35.7 1.2 %collective-permute-start.7 = (f32[128,256]{1,0:T(8,128)S(1)}, f32[128,256]{1,0:T(8,128)S(1)}, u32[]{:S(2)}, u32[]{:S(2)}) collective-permute-start(f32[128,256]{1,0:T(8,128)S(1)} %get-tuple-element.25), channel_id=1, source_target_pairs={{0,16},{8,24},{16,0},{24,8},{1,17},{9,25},{17,1},{25,9},{2,18},{10... | collective-permute-start | bytes 393224 | tf_op jit(solution)/shard_map/ppermute | solution.py:289
  36.9 0.8 %collective-permute-start.8 = (f32[128,256]{1,0:T(8,128)S(1)}, f32[128,256]{1,0:T(8,128)S(1)}, u32[]{:S(2)}, u32[]{:S(2)}) collective-permute-start(f32[128,256]{1,0:T(8,128)S(1)} %get-tuple-element.26), channel_id=1, source_target_pairs={{0,24},{8,16},{16,8},{24,0},{1,25},{9,17},{17,9},{25,1},{2,26},{10... | collective-permute-start | bytes 393224 | tf_op jit(solution)/shard_map/ppermute | solution.py:289
  37.7 2.4 %collective-permute-done.6 = f32[128,256]{1,0:T(8,128)S(1)} collective-permute-done((f32[128,256]{1,0:T(8,128)S(1)}, f32[128,256]{1,0:T(8,128)S(1)}, u32[]{:S(2)}, u32[]{:S(2)}) %collective-permute-start.6) | collective-permute-done | bytes 131104 | tf_op jit(solution)/shard_map/ppermute | solution.py:289
  40.2 3.6 %collective-permute-done.7 = f32[128,256]{1,0:T(8,128)S(1)} collective-permute-done((f32[128,256]{1,0:T(8,128)S(1)}, f32[128,256]{1,0:T(8,128)S(1)}, u32[]{:S(2)}, u32[]{:S(2)}) %collective-permute-start.7) | collective-permute-done | bytes 131104 | tf_op jit(solution)/shard_map/ppermute | solution.py:289
  43.8 0.0 collective-permute-done.8
  43.8 0.1 collective-permute-start.9
  43.9 1.3 %collective-permute-done.9 = f32[128,256]{1,0:T(8,128)S(1)} collective-permute-done((f32[128,256]{1,0:T(8,128)S(1)}, f32[128,256]{1,0:T(8,128)S(1)}, u32[]{:S(2)}, u32[]{:S(2)}) %collective-permute-start.9) | collective-permute-done | bytes 131104 | tf_op jit(solution)/shard_map/ppermute | solution.py:292
  45.3 0.7 %maximum_bitcast_fusion = f32[1,128,512]{2,1,0:T(8,128)} fusion(f32[128,256]{1,0:T(8,128)S(1)} %get-tuple-element.28, f32[128,256]{1,0:T(8,128)S(1)} %get-tuple-element.27), kind=kLoop, calls=%fused_computation | loop fusion | flops 65536 | bytes 524288 | tf_op jit(solution)/shard_map/broadcast_in_dim | solution.py:300
  (2 shorter events, 0.1 us)
Async XLA Ops:
  0.0 17.6 %collective-permute-start = (bf16[512,256]{1,0:T(8,128)(2,1)}, bf16[512,256]{1,0:T(8,128)(2,1)S(1)}, u32[]{:S(2)}, u32[]{:S(2)}) collective-permute-start(bf16[512,256]{1,0:T(8,128)(2,1)} %own_hbm.1), channel_id=1, source_target_pairs={{0,2},{2,0},{4,6},{6,4},{1,3},{3,1},{5,7},{7,5},{8,10},{10,8},{12,... | collective-permute-start | bytes 786440 | tf_op jit(solution)/shard_map/ppermute | solution.py:199
  4.0 7.6 %collective-permute-start.1 = (bf16[256,256]{1,0:T(8,128)(2,1)S(1)}, bf16[256,256]{1,0:T(8,128)(2,1)S(1)}, u32[]{:S(2)}, u32[]{:S(2)}) collective-permute-start(bf16[256,256]{1,0:T(8,128)(2,1)S(1)} %constant_dynamic-slice_fusion), channel_id=1, source_target_pairs={{0,4},{2,6},{4,0},{6,2},{8,12},{10,14},{12,8},{14,10},{16,22},{18,... | collective-permute-start | bytes 393224 | tf_op jit(solution)/shard_map/ppermute | solution.py:198
  11.6 12.0 %collective-permute-start.4 = (bf16[256,256]{1,0:T(8,128)(2,1)S(1)}, bf16[256,256]{1,0:T(8,128)(2,1)S(1)}, u32[]{:S(2)}, u32[]{:S(2)}) collective-permute-start(bf16[256,256]{1,0:T(8,128)(2,1)S(1)} %collective-permute-done.1.chunk_ref), channel_id=1, source_target_pairs={{0,8},{8,0},{16,24},{24,16},{1,9},{9,1},{17,25},{25,17},{2,10},{10... | collective-permute-start | bytes 393224 | tf_op jit(solution)/shard_map/ppermute | solution.py:202
  13.1 12.2 %collective-permute-start.3 = (bf16[256,256]{1,0:T(8,128)(2,1)S(1)}, bf16[256,256]{1,0:T(8,128)(2,1)S(1)}, u32[]{:S(2)}, u32[]{:S(2)}) collective-permute-start(bf16[256,256]{1,0:T(8,128)(2,1)S(1)} %collective-permute-done.1.chunk_ref), channel_id=1, source_target_pairs={{0,16},{8,24},{16,0},{24,8},{1,17},{9,25},{17,1},{25,9},{2,18},{10... | collective-permute-start | bytes 393224 | tf_op jit(solution)/shard_map/ppermute | solution.py:202
  17.6 10.9 %collective-permute-start.2 = (bf16[256,256]{1,0:T(8,128)(2,1)S(1)}, bf16[256,256]{1,0:T(8,128)(2,1)S(1)}, u32[]{:S(2)}, u32[]{:S(2)}) collective-permute-start(bf16[256,256]{1,0:T(8,128)(2,1)S(1)} %collective-permute-done.1.chunk_ref), channel_id=1, source_target_pairs={{0,24},{8,16},{16,8},{24,0},{1,25},{9,17},{17,9},{25,1},{2,26},{10... | collective-permute-start | bytes 393224 | tf_op jit(solution)/shard_map/ppermute | solution.py:202
  32.1 2.0 %collective-permute-start.5 = (f32[512,256]{1,0:T(8,128)S(1)}, f32[512,256]{1,0:T(8,128)S(1)}, u32[]{:S(2)}, u32[]{:S(2)}) collective-permute-start(f32[512,256]{1,0:T(8,128)S(1)} %get-tuple-element.22), channel_id=1, source_target_pairs={{0,1},{1,0},{2,3},{3,2},{4,5},{5,4},{6,7},{7,6},{8,9},{9,8},{10,11... | collective-permute-start | bytes 1572872 | tf_op jit(solution)/shard_map/ppermute | solution.py:276
  34.2 6.0 %collective-permute-start.6 = (f32[128,256]{1,0:T(8,128)S(1)}, f32[128,256]{1,0:T(8,128)S(1)}, u32[]{:S(2)}, u32[]{:S(2)}) collective-permute-start(f32[128,256]{1,0:T(8,128)S(1)} %get-tuple-element.24), channel_id=1, source_target_pairs={{0,8},{8,0},{16,24},{24,16},{1,9},{9,1},{17,25},{25,17},{2,10},{10... | collective-permute-start | bytes 393224 | tf_op jit(solution)/shard_map/ppermute | solution.py:289
  35.7 8.1 %collective-permute-start.7 = (f32[128,256]{1,0:T(8,128)S(1)}, f32[128,256]{1,0:T(8,128)S(1)}, u32[]{:S(2)}, u32[]{:S(2)}) collective-permute-start(f32[128,256]{1,0:T(8,128)S(1)} %get-tuple-element.25), channel_id=1, source_target_pairs={{0,16},{8,24},{16,0},{24,8},{1,17},{9,25},{17,1},{25,9},{2,18},{10... | collective-permute-start | bytes 393224 | tf_op jit(solution)/shard_map/ppermute | solution.py:289
  36.9 6.9 %collective-permute-start.8 = (f32[128,256]{1,0:T(8,128)S(1)}, f32[128,256]{1,0:T(8,128)S(1)}, u32[]{:S(2)}, u32[]{:S(2)}) collective-permute-start(f32[128,256]{1,0:T(8,128)S(1)} %get-tuple-element.26), channel_id=1, source_target_pairs={{0,24},{8,16},{16,8},{24,0},{1,25},{9,17},{17,9},{25,1},{2,26},{10... | collective-permute-start | bytes 393224 | tf_op jit(solution)/shard_map/ppermute | solution.py:289
  43.8 1.4 %collective-permute-start.9 = (f32[128,256]{1,0:T(8,128)S(1)}, f32[128,256]{1,0:T(8,128)S(1)}, u32[]{:S(2)}, u32[]{:S(2)}) collective-permute-start(f32[128,256]{1,0:T(8,128)S(1)} %add_multiply_fusion), channel_id=1, source_target_pairs={{0,1},{1,0},{2,3},{3,2},{4,5},{5,4},{6,7},{7,6},{8,9},{9,8},{10,11... | collective-permute-start | bytes 393224 | tf_op jit(solution)/shard_map/ppermute | solution.py:292

commit v2 on v1

v2 whole, which is shorter than its diff:
```python
import functools
import math

import jax
import jax.numpy as jnp
from jax import lax
from jax.experimental import pallas as pl
from jax.experimental.pallas import tpu as pltpu
from jax.sharding import PartitionSpec as P


ANY = pl.BlockSpec(memory_space=pl.ANY)
VMEM = pl.BlockSpec(memory_space=pltpu.VMEM)
SMEM = pl.BlockSpec(memory_space=pltpu.SMEM)
HBM = pl.BlockSpec(memory_space=pltpu.HBM)


def exchange_pairs(distance, size):
    return [(i, i ^ distance) for i in range(size)]


def in_hbm(x):
    return pltpu.with_memory_space_constraint(x, pltpu.HBM)


def add_slot(table, i, ints_ref, coef, acc_ref):
    aux_total, _, _, width, _ = ints_ref.shape
    left = ints_ref[:, 0, table[i]].reshape(aux_total * width, width)
    product = jnp.dot(left, coef, preferred_element_type=jnp.float32)
    acc_ref[...] += product.reshape(acc_ref.shape)


def head_kernel(piece, t, coef_hbm, out_ref, sem):
    width = coef_hbm.shape[0]
    depth = (lax.axis_size("blk") - 2) * width // lax.axis_size("aux")
    start = lax.rem(lax.axis_index("aux") * depth + t * piece, width)
    rows = pl.ds(pl.multiple_of(start, piece), piece)
    copy = pltpu.make_async_copy(coef_hbm.at[rows], out_ref, sem)
    copy.start()
    copy.wait()


def own_kernel(counts, lists_hbm, ints_ref, coef_hbm, acc_ref, table, coef, lists, sems):
    slot_total = ints_ref.shape[2]
    lists_copy = pltpu.make_async_copy(lists_hbm, lists, sems.at[0])
    lists_copy.start()
    coef_copy = pltpu.make_async_copy(coef_hbm, coef, sems.at[1])
    coef_copy.start()
    acc_ref[...] = jnp.zeros_like(acc_ref)
    lists_copy.wait()
    me = lax.axis_index("blk")
    live = counts[0]
    found = jnp.int32(0)
    for step, (lo, hi) in enumerate(((0, 1), (1, 2), (2, 1 << 30))):
        for slot in range(slot_total):
            away = lists[0, slot] ^ me
            table[found] = slot
            table[slot_total + 1 + found] = away
            found = found + ((slot < live) & (away >= lo) & (away < hi)).astype(jnp.int32)
        table[2 * slot_total + 2 + step] = found
    coef_copy.wait()

    @pl.loop(0, table[2 * slot_total + 2])
    def _(i):
        add_slot(table, i, ints_ref, coef[...], acc_ref)


def next_kernel(table, ints_ref, next_ref, _acc, acc_ref):
    slot_total = ints_ref.shape[2]

    @pl.loop(table[2 * slot_total + 2], table[2 * slot_total + 3])
    def _(i):
        add_slot(table, i, ints_ref, next_ref[...], acc_ref)


def add_far(distances, complete_after, table, ints_ref, chunks, coef, acc_ref):
    _, _, slot_total, width, _ = ints_ref.shape
    depth = chunks[0].shape[0]
    piece = math.gcd(depth, width)
    me = lax.axis_index("aux")
    for k, chunk in enumerate(chunks):
        if k in complete_after:
            rows = pl.ds(pl.multiple_of((me ^ k) * depth, depth), depth)
            coef[rows, :] = chunk[...]

    @pl.loop(table[2 * slot_total + 3], table[2 * slot_total + 4])
    def _(i):
        start = (table[slot_total + 1 + i] - 2) * width
        last = jnp.int32(0)
        for part in range(width // piece):
            last = jnp.maximum(last, ((start + part * piece) // depth) ^ me)

        @pl.when((last >= distances[0]) & (last <= distances[-1]))
        def _():
            rows = pl.ds(pl.multiple_of(start, width), width)
            add_slot(table, i, ints_ref, coef[rows, :], acc_ref)


def far_kernel(distances, needed, table, ints_ref, *rest):
    *chunks, _, acc_ref, coef = rest
    add_far(distances, needed, table, ints_ref, chunks, coef, acc_ref)


def last_kernel(distances, needed, occ_size, table, ints_ref, *rest):
    *chunks, _, acc_ref, halves = rest[: -occ_size]
    pieces, coef = rest[-occ_size:-1], rest[-1]
    add_far(distances, needed, table, ints_ref, chunks, coef, acc_ref)
    columns = acc_ref.shape[2]
    for p in range(acc_ref.shape[0]):
        halves[:, p * columns : (p + 1) * columns] = acc_ref[p].astype(jnp.bfloat16)
    for k, piece_ref in enumerate(pieces, 1):
        share_kernel(k, halves, piece_ref)


def share_kernel(distance, halves, piece_ref):
    share = piece_ref.shape[1]
    start = (lax.axis_index("occ") ^ distance) * share
    rows = pl.ds(pl.multiple_of(start, share), share)
    piece_ref[...] = lax.dot_general(
        halves[...], halves[rows, :], (((1,), (1,)), ((), ())), preferred_element_type=jnp.float32
    )


def split_kernel(*refs):
    aux_size, occ_size = lax.axis_size("aux"), lax.axis_size("occ")
    terms, outs = refs[:occ_size], refs[occ_size:]
    my_aux = lax.axis_index("aux")
    depth = outs[0].shape[0]
    for k in range(aux_size):
        rows = pl.ds(pl.multiple_of((my_aux ^ k) * depth, depth), depth)
        total = terms[0][rows, :]
        for term in terms[1:]:
            total = total + term[rows, :]
        outs[k][...] = total


def per_device(integrals, orbitals, pair_lists, pair_counts):
    aux_total, _, slot_total, width, _ = integrals.shape
    columns = orbitals.shape[1]
    aux_size, blk_size, occ_size = (lax.axis_size(n) for n in ("aux", "blk", "occ"))
    my_occ = lax.axis_index("occ")
    slot_flops = 2 * aux_total * width * width * columns
    slot_bytes = 2 * aux_total * width * width

    def cost(slots):
        return pl.CostEstimate(
            flops=slots * slot_flops, bytes_accessed=slots * slot_bytes, transcendentals=0
        )

    depth = (blk_size - 2) * width // aux_size
    piece = math.gcd(depth, width)
    parts = []
    for t in range(depth // piece):
        starts = [a * depth + t * piece for a in range(aux_size)]
        pairs = [
            (a * blk_size + i, a * blk_size + (i ^ (2 + starts[a] // width)))
            for a in range(aux_size)
            for i in range(blk_size)
        ]
        sent = pl.pallas_call(
            functools.partial(head_kernel, piece, t),
            out_shape=jax.ShapeDtypeStruct((piece, columns), orbitals.dtype),
            in_specs=[HBM],
            out_specs=VMEM,
            scratch_shapes=[pltpu.SemaphoreType.DMA],
            compiler_params=pltpu.CompilerParams(vmem_limit_bytes=1 << 20),
            cost_estimate=cost(8 * slot_total),
            name="head",
        )(in_hbm(orbitals))
        parts.append(lax.ppermute(sent, ("aux", "blk"), pairs))
    next_block = lax.ppermute(orbitals, "blk", exchange_pairs(1, blk_size))
    chunk = parts[0] if len(parts) == 1 else jnp.concatenate(parts, 0)
    chunks = [chunk] + [
        lax.ppermute(chunk, "aux", exchange_pairs(k, aux_size)) for k in range(1, aux_size)
    ]

    acc_shape = jax.ShapeDtypeStruct((aux_total, width, columns), jnp.float32)
    table_shape = jax.ShapeDtypeStruct((2 * slot_total + 5,), jnp.int32)
    small = pltpu.CompilerParams(vmem_limit_bytes=8 << 20)
    ints = integrals

    acc, table = pl.pallas_call(
        own_kernel,
        out_shape=(acc_shape, table_shape),
        in_specs=[SMEM, HBM, VMEM, HBM],
        out_specs=(VMEM, SMEM),
        scratch_shapes=[
            pltpu.VMEM((width, columns), jnp.bfloat16),
            pltpu.SMEM(pair_lists.shape, jnp.int32),
            pltpu.SemaphoreType.DMA((2,)),
        ],
        compiler_params=small,
        cost_estimate=cost(3),
        name="own",
    )(pair_counts, in_hbm(pair_lists), ints, in_hbm(orbitals))
    acc = pl.pallas_call(
        next_kernel,
        out_shape=acc_shape,
        in_specs=[SMEM, VMEM, VMEM, VMEM],
        out_specs=VMEM,
        input_output_aliases={3: 0},
        compiler_params=small,
        cost_estimate=cost(3),
        name="next",
    )(table, ints, next_block, acc)

    share = width // occ_size
    piece_shape = jax.ShapeDtypeStruct((width, share), jnp.float32)
    halves_shape = jax.ShapeDtypeStruct((width, aux_total * columns), jnp.bfloat16)
    far_scratch = [pltpu.VMEM((aux_size * depth, columns), jnp.bfloat16)]
    far_params = pltpu.CompilerParams(
        vmem_limit_bytes=(6 << 20) + 2 * columns * depth * aux_size
    )
    whole_pairs = (2 * depth) % width == 0
    acc = pl.pallas_call(
        functools.partial(far_kernel, (0, 1), (0, 1)),
        out_shape=acc_shape,
        in_specs=[SMEM] + [VMEM] * 4,
        out_specs=VMEM,
        scratch_shapes=far_scratch,
        input_output_aliases={4: 0},
        compiler_params=far_params,
        cost_estimate=cost(3),
        name="far",
    )(table, ints, *chunks[:2], acc)
    needed = tuple(range(2 if whole_pairs else 0, aux_size))
    _, halves, *pieces = pl.pallas_call(
        functools.partial(last_kernel, (2, aux_size - 1), needed, occ_size),
        out_shape=[acc_shape, halves_shape] + [piece_shape] * (occ_size - 1),
        in_specs=[SMEM, VMEM] + [VMEM] * (aux_size + 1),
        out_specs=[VMEM] * (occ_size + 1),
        scratch_shapes=far_scratch,
        input_output_aliases={aux_size + 2: 0},
        compiler_params=far_params,
        cost_estimate=cost(3),
        name="last",
    )(table, ints, *chunks, acc)
    kept = pl.pallas_call(
        functools.partial(share_kernel, 0),
        out_shape=piece_shape,
        in_specs=[VMEM],
        out_specs=VMEM,
        compiler_params=small,
        cost_estimate=cost(1),
        name="kept",
    )(halves)

    terms = [kept] + [
        lax.ppermute(pieces[k - 1], "occ", exchange_pairs(k, occ_size)) for k in range(1, occ_size)
    ]
    rows = width // aux_size
    mine = pl.pallas_call(
        split_kernel,
        out_shape=[jax.ShapeDtypeStruct((rows, share), jnp.float32)] * aux_size,
        in_specs=[VMEM] * occ_size,
        out_specs=[VMEM] * aux_size,
        compiler_params=pltpu.CompilerParams(vmem_limit_bytes=8 << 20),
        name="split",
    )(*terms)
    total = mine[0]
    for k in range(1, aux_size):
        total = total + lax.ppermute(mine[k], "aux", exchange_pairs(k, aux_size))
    total = total / (columns * occ_size)
    shares = [total] + [
        lax.ppermute(total, "occ", exchange_pairs(k, occ_size)) for k in range(1, occ_size)
    ]
    ordered = []
    for o in range(occ_size):
        value = shares[0]
        for k in range(1, occ_size):
            value = jnp.where((my_occ ^ k) == o, shares[k], value)
        ordered.append(value)
    return jnp.concatenate(ordered, 1)[None]


def solution(mesh):
    placed = (P("aux", "blk", None, None, None), P("blk", "occ"), P("blk", None), P("blk"))
    return jax.shard_map(
        per_device, mesh=mesh, in_specs=placed, out_specs=P("blk", "aux", None), check_vma=False
    )
```

time: 46.2 us -> 41.7 us (0.903)
  Pallas kernels: 19 us -> 12.9 us
  starting transfers between devices: 15.3 us -> 13.3 us
  local copies, waits for them, and re-layouts: 0.95 us -> 2.52 us
  waiting for transfers between devices: 9.12 us -> 10.5 us
  between operations: 0.77 us -> 1.5 us
    pallas_call x5, Pallas kernels: 18.5 us -> 12.4 us  [the longest x1 4.91 us: per_device(): pl.pallas_call(functools.partial(last_kernel, (2, aux_size - 1), needed,...]
    unnamed x0 -> x2, local copies, waits for them, and re-layouts: none -> 2.52 us
    ppermute x3, waiting for transfers between devices: 0.01 us -> 2.42 us  [per_device(): lax.ppermute(chunk, 'aux', exchange_pairs(k, aux_size))]
    ppermute x3, starting transfers between devices: 5.94 us -> 3.89 us  [per_device(): lax.ppermute(chunk, 'aux', exchange_pairs(k, aux_size))]
    dynamic_slice x1 -> x0, local copies, waits for them, and re-layouts: 0.95 us -> none  [per_device(): sent = lax.dynamic_slice_in_dim(orbitals, offset, piece, 0)]
    ppermute x3, waiting for transfers between devices: 6.08 us -> 5.36 us  [per_device(): total = total + lax.ppermute(mine[k], 'aux', exchange_pairs(k, aux_size))]
  transfers between devices with their start and end apart: 10 -> 10, of which waited for: 5 -> 7; matrix products, arithmetic and copies ran while one was open for 2% -> 0% of each run, Pallas kernels for 33% -> 19%
where the time goes in v2:
time: 41.7 us; the launch traced here: 41.5 us
  starting transfers between devices  13.3 us (32%)
  Pallas kernels  12.9 us (31%)
  waiting for transfers between devices  10.5 us (25%)
  local copies, waits for them, and re-layouts  2.52 us (6%)
  between operations  1.5 us (4%)
  other arithmetic  0.78 us (2%)
    ppermute x3, waiting for transfers between devices, per_device(): total = total + lax.ppermute(mine[k], 'aux', exchange_pairs(k, aux_size))  5.36 us
    pallas_call x1, Pallas kernels, per_device(): pl.pallas_call(functools.partial(last_kernel, (2, aux_size - 1), needed,...  4.91 us
    ppermute x3, starting transfers between devices, per_device(): lax.ppermute(chunk, 'aux', exchange_pairs(k, aux_size))  3.89 us
    ppermute x3, starting transfers between devices, per_device(): total = total + lax.ppermute(mine[k], 'aux', exchange_pairs(k, aux_size))  3.55 us
    ppermute x1, starting transfers between devices, per_device(): next_block = lax.ppermute(orbitals, 'blk', exchange_pairs(1, blk_size))  3.05 us
    pallas_call x1, Pallas kernels, per_device(): pl.pallas_call(own_kernel, out_shape=(acc_shape, table_shape), in_specs=[...  2.98 us
    ppermute x1, starting transfers between devices, per_device(): parts.append(lax.ppermute(sent, ('aux', 'blk'), pairs))  2.65 us
    unnamed x2, local copies, waits for them, and re-layouts  2.52 us
  transfers between devices with their start and end apart: 10, of which 7 were waited for; matrix products, arithmetic and copies ran while one was open for 0% of the time, Pallas kernels for 19%

profile of v2, /device:TPU:0, one launch (start us, length us, event | category | flops | bytes accessed | tf_op | source)
XLA Modules:
  0.0 41.5 jit_solution(4397696455284871466)
XLA Ops:
  0.0 3.1 %collective-permute-start.4 = (bf16[512,256]{1,0:T(8,128)(2,1)}, bf16[512,256]{1,0:T(8,128)(2,1)S(1)}, u32[]{:S(2)}, u32[]{:S(2)}) collective-permute-start(bf16[512,256]{1,0:T(8,128)(2,1)} %coef_hbm.3), channel_id=1, source_target_pairs={{0,2},{2,0},{4,6},{6,4},{1,3},{3,1},{5,7},{7,5},{8,10},{10,8},{12,... | collective-permute-start | bytes 786440 | tf_op jit(solution)/shard_map/ppermute | solution.py:171
  3.1 0.0 copy-start
  3.1 1.1 %head.1 = bf16[256,256]{1,0:T(8,128)(2,1)S(1)} custom-call(bf16[512,256]{1,0:T(8,128)(2,1)} %coef_hbm.3), custom_call_target="tpu_custom_call" | custom-call | flops 47244640256 | bytes 184549376 | tf_op jit(solution)/shard_map/head/pallas_call | solution.py:160
  4.1 2.7 %collective-permute-start = (bf16[256,256]{1,0:T(8,128)(2,1)S(1)}, bf16[256,256]{1,0:T(8,128)(2,1)S(1)}, u32[]{:S(2)}, u32[]{:S(2)}) collective-permute-start(bf16[256,256]{1,0:T(8,128)(2,1)S(1)} %head.1), channel_id=1, source_target_pairs={{0,4},{2,6},{4,0},{6,2},{8,12},{10,14},{12,8},{14,10},{16,22},{18,... | collective-permute-start | bytes 393224 | tf_op jit(solution)/shard_map/ppermute | solution.py:170
  8.2 2.5 %copy-done = bf16[4,1,11,512,512]{4,3,2,1,0:T(8,128)(2,1)S(1)} copy-done((bf16[4,1,11,512,512]{4,3,2,1,0:T(8,128)(2,1)S(1)}, bf16[4,1,11,512,512]{4,3,2,1,0:T(8,128)(2,1)}, u32[]{:S(2)}) %copy-start) | copy-done | bytes 23068696
  10.7 3.0 %own.1 = (f32[4,512,256]{2,1,0:T(8,128)S(1)}, s32[27]{0:T(128)S(1)}) custom-call(s32[1]{0:T(128)S(6)} %copy.11.counts, s32[1,11]{1,0:T(1,128)} %lists_hbm.1, bf16[4,1,11,512,512]{4,3,2,1,0:T(8,128)(2,1)S(1)} %copy-done, bf16[512,256]{1,0:T(8,128)(2,1)} %coef_hbm.3), custom_call_target="tpu_custom_call" | custom-call | flops 1610612736 | bytes 6291456 | tf_op jit(solution)/shard_map/own/pallas_call | solution.py:182
  13.7 0.0 collective-permute-done.rest_0_
  13.7 1.6 %collective-permute-start.1 = (bf16[256,256]{1,0:T(8,128)(2,1)S(1)}, bf16[256,256]{1,0:T(8,128)(2,1)S(1)}, u32[]{:S(2)}, u32[]{:S(2)}) collective-permute-start(bf16[256,256]{1,0:T(8,128)(2,1)S(1)} %collective-permute-done.rest_0_), channel_id=1, source_target_pairs={{0,8},{8,0},{16,24},{24,16},{1,9},{9,1},{17,25},{25,17},{2,10},{10... | collective-permute-start | bytes 393224 | tf_op jit(solution)/shard_map/ppermute | solution.py:174
  15.2 2.3 %collective-permute-start.2 = (bf16[256,256]{1,0:T(8,128)(2,1)S(1)}, bf16[256,256]{1,0:T(8,128)(2,1)S(1)}, u32[]{:S(2)}, u32[]{:S(2)}) collective-permute-start(bf16[256,256]{1,0:T(8,128)(2,1)S(1)} %collective-permute-done.rest_0_), channel_id=1, source_target_pairs={{0,16},{8,24},{16,0},{24,8},{1,17},{9,25},{17,1},{25,9},{2,18},{10... | collective-permute-start | bytes 393224 | tf_op jit(solution)/shard_map/ppermute | solution.py:174
  17.6 0.0 collective-permute-start.3
  17.6 0.0 collective-permute-done.4.next_ref
  17.6 1.2 %next.1.rest_2_ = f32[4,512,256]{2,1,0:T(8,128)S(1)} custom-call(s32[27]{0:T(128)S(1)} %get-tuple-element.13.table, bf16[4,1,11,512,512]{4,3,2,1,0:T(8,128)(2,1)S(1)} %copy-done, bf16[512,256]{1,0:T(8,128)(2,1)S(1)} %collective-permute-done.4.next_ref, f32[4,512,256]{2,1,0:T(8,128)S(1)} %get-tuple-element.14._acc), custom_call_target="tpu_custom_call", output_to_operand_aliasing={{}: (3, {})} | custom-call | flops 1610612736 | bytes 6291456 | tf_op jit(solution)/shard_map/next/pallas_call | solution.py:196
  18.8 0.3 collective-permute-done.1.rest_1_
  19.1 2.2 %far.1.rest_4_ = f32[4,512,256]{2,1,0:T(8,128)S(1)} custom-call(s32[27]{0:T(128)S(1)} %get-tuple-element.13.table, bf16[4,1,11,512,512]{4,3,2,1,0:T(8,128)(2,1)S(1)} %copy-done, bf16[256,256]{1,0:T(8,128)(2,1)S(1)} %collective-permute-done.rest_0_, bf16[256,256]{1,0:T(8,128)(2,1)S(1)} %collective-permute-done.1.rest_1_, ...), custom_call_target="tpu_custom_call", output_to_operand_aliasing={{}: (4, {})} | custom-call | flops 1610612736 | bytes 6291456 | tf_op jit(solution)/shard_map/far/pallas_call | solution.py:215
  21.3 0.7 %collective-permute-done.2.rest_2_ = bf16[256,256]{1,0:T(8,128)(2,1)S(1)} collective-permute-done((bf16[256,256]{1,0:T(8,128)(2,1)S(1)}, bf16[256,256]{1,0:T(8,128)(2,1)S(1)}, u32[]{:S(2)}, u32[]{:S(2)}) %collective-permute-start.2) | collective-permute-done | bytes 131104 | tf_op jit(solution)/shard_map/ppermute | solution.py:174
  22.0 1.4 %collective-permute-done.3.rest_3_ = bf16[256,256]{1,0:T(8,128)(2,1)S(1)} collective-permute-done((bf16[256,256]{1,0:T(8,128)(2,1)S(1)}, bf16[256,256]{1,0:T(8,128)(2,1)S(1)}, u32[]{:S(2)}, u32[]{:S(2)}) %collective-permute-start.3) | collective-permute-done | bytes 131104 | tf_op jit(solution)/shard_map/ppermute | solution.py:174
  23.4 4.9 %last.1 = (f32[4,512,256]{2,1,0:T(8,128)S(1)}, bf16[512,1024]{1,0:T(8,128)(2,1)S(1)}, f32[512,256]{1,0:T(8,128)S(1)}) custom-call(s32[27]{0:T(128)S(1)} %get-tuple-element.13.table, bf16[4,1,11,512,512]{4,3,2,1,0:T(8,128)(2,1)S(1)} %copy-done, bf16[256,256]{1,0:T(8,128)(2,1)S(1)} %collective-permute-done.rest_0_, ...), custom_call_target="tpu_custom_call", output_to_operand_aliasing={{0}: (6, {})} | custom-call | flops 1610612736 | bytes 6291456 | tf_op jit(solution)/shard_map/last/pallas_call | solution.py:227
  28.4 0.1 collective-permute-start.5
  28.4 0.5 %kept.1.refs_0_ = f32[512,256]{1,0:T(8,128)S(1)} custom-call(bf16[512,1024]{1,0:T(8,128)(2,1)S(1)} %get-tuple-element.15.halves), custom_call_target="tpu_custom_call" | custom-call | flops 536870912 | bytes 2097152 | tf_op jit(solution)/shard_map/kept/pallas_call | solution.py:238
  28.9 1.4 %collective-permute-done.5.refs_1_ = f32[512,256]{1,0:T(8,128)S(1)} collective-permute-done((f32[512,256]{1,0:T(8,128)S(1)}, f32[512,256]{1,0:T(8,128)S(1)}, u32[]{:S(2)}, u32[]{:S(2)}) %collective-permute-start.5) | collective-permute-done | bytes 524320 | tf_op jit(solution)/shard_map/ppermute | solution.py:249
  30.3 0.1 split.1
  30.4 0.8 %collective-permute-start.6 = (f32[128,256]{1,0:T(8,128)S(1)}, f32[128,256]{1,0:T(8,128)S(1)}, u32[]{:S(2)}, u32[]{:S(2)}) collective-permute-start(f32[128,256]{1,0:T(8,128)S(1)} %get-tuple-element.18), channel_id=1, source_target_pairs={{0,8},{8,0},{16,24},{24,16},{1,9},{9,1},{17,25},{25,17},{2,10},{10... | collective-permute-start | bytes 393224 | tf_op jit(solution)/shard_map/ppermute | solution.py:262
  31.3 1.4 %collective-permute-start.7 = (f32[128,256]{1,0:T(8,128)S(1)}, f32[128,256]{1,0:T(8,128)S(1)}, u32[]{:S(2)}, u32[]{:S(2)}) collective-permute-start(f32[128,256]{1,0:T(8,128)S(1)} %get-tuple-element.19), channel_id=1, source_target_pairs={{0,16},{8,24},{16,0},{24,8},{1,17},{9,25},{17,1},{25,9},{2,18},{10... | collective-permute-start | bytes 393224 | tf_op jit(solution)/shard_map/ppermute | solution.py:262
  32.6 1.3 %collective-permute-start.8 = (f32[128,256]{1,0:T(8,128)S(1)}, f32[128,256]{1,0:T(8,128)S(1)}, u32[]{:S(2)}, u32[]{:S(2)}) collective-permute-start(f32[128,256]{1,0:T(8,128)S(1)} %get-tuple-element.20), channel_id=1, source_target_pairs={{0,24},{8,16},{16,8},{24,0},{1,25},{9,17},{17,9},{25,1},{2,26},{10... | collective-permute-start | bytes 393224 | tf_op jit(solution)/shard_map/ppermute | solution.py:262
  34.0 2.9 %collective-permute-done.6 = f32[128,256]{1,0:T(8,128)S(1)} collective-permute-done((f32[128,256]{1,0:T(8,128)S(1)}, f32[128,256]{1,0:T(8,128)S(1)}, u32[]{:S(2)}, u32[]{:S(2)}) %collective-permute-start.6) | collective-permute-done | bytes 131104 | tf_op jit(solution)/shard_map/ppermute | solution.py:262
  36.8 2.5 %collective-permute-done.7 = f32[128,256]{1,0:T(8,128)S(1)} collective-permute-done((f32[128,256]{1,0:T(8,128)S(1)}, f32[128,256]{1,0:T(8,128)S(1)}, u32[]{:S(2)}, u32[]{:S(2)}) %collective-permute-start.7) | collective-permute-done | bytes 131104 | tf_op jit(solution)/shard_map/ppermute | solution.py:262
  39.3 0.0 collective-permute-done.8
  39.4 0.1 collective-permute-start.9
  39.4 1.3 %collective-permute-done.9 = f32[128,256]{1,0:T(8,128)S(1)} collective-permute-done((f32[128,256]{1,0:T(8,128)S(1)}, f32[128,256]{1,0:T(8,128)S(1)}, u32[]{:S(2)}, u32[]{:S(2)}) %collective-permute-start.9) | collective-permute-done | bytes 131104 | tf_op jit(solution)/shard_map/ppermute | solution.py:265
  40.8 0.7 %maximum_bitcast_fusion = f32[1,128,512]{2,1,0:T(8,128)} fusion(f32[128,256]{1,0:T(8,128)S(1)} %get-tuple-element.22, f32[128,256]{1,0:T(8,128)S(1)} %get-tuple-element.21), kind=kLoop, calls=%fused_computation | loop fusion | flops 65536 | bytes 524288 | tf_op jit(solution)/shard_map/broadcast_in_dim | solution.py:273
  (2 shorter events, 0.1 us)
Async XLA Ops:
  0.0 17.6 %collective-permute-start.4 = (bf16[512,256]{1,0:T(8,128)(2,1)}, bf16[512,256]{1,0:T(8,128)(2,1)S(1)}, u32[]{:S(2)}, u32[]{:S(2)}) collective-permute-start(bf16[512,256]{1,0:T(8,128)(2,1)} %coef_hbm.3), channel_id=1, source_target_pairs={{0,2},{2,0},{4,6},{6,4},{1,3},{3,1},{5,7},{7,5},{8,10},{10,8},{12,... | collective-permute-start | bytes 786440 | tf_op jit(solution)/shard_map/ppermute | solution.py:171
  3.1 7.6 %copy-start = (bf16[4,1,11,512,512]{4,3,2,1,0:T(8,128)(2,1)S(1)}, bf16[4,1,11,512,512]{4,3,2,1,0:T(8,128)(2,1)}, u32[]{:S(2)}) copy-start(bf16[4,1,11,512,512]{4,3,2,1,0:T(8,128)(2,1)} %ints_ref.7) | copy-start | bytes 69206016
  4.1 9.6 %collective-permute-start = (bf16[256,256]{1,0:T(8,128)(2,1)S(1)}, bf16[256,256]{1,0:T(8,128)(2,1)S(1)}, u32[]{:S(2)}, u32[]{:S(2)}) collective-permute-start(bf16[256,256]{1,0:T(8,128)(2,1)S(1)} %head.1), channel_id=1, source_target_pairs={{0,4},{2,6},{4,0},{6,2},{8,12},{10,14},{12,8},{14,10},{16,22},{18,... | collective-permute-start | bytes 393224 | tf_op jit(solution)/shard_map/ppermute | solution.py:170
  13.7 5.4 %collective-permute-start.1 = (bf16[256,256]{1,0:T(8,128)(2,1)S(1)}, bf16[256,256]{1,0:T(8,128)(2,1)S(1)}, u32[]{:S(2)}, u32[]{:S(2)}) collective-permute-start(bf16[256,256]{1,0:T(8,128)(2,1)S(1)} %collective-permute-done.rest_0_), channel_id=1, source_target_pairs={{0,8},{8,0},{16,24},{24,16},{1,9},{9,1},{17,25},{25,17},{2,10},{10... | collective-permute-start | bytes 393224 | tf_op jit(solution)/shard_map/ppermute | solution.py:174
  15.2 6.8 %collective-permute-start.2 = (bf16[256,256]{1,0:T(8,128)(2,1)S(1)}, bf16[256,256]{1,0:T(8,128)(2,1)S(1)}, u32[]{:S(2)}, u32[]{:S(2)}) collective-permute-start(bf16[256,256]{1,0:T(8,128)(2,1)S(1)} %collective-permute-done.rest_0_), channel_id=1, source_target_pairs={{0,16},{8,24},{16,0},{24,8},{1,17},{9,25},{17,1},{25,9},{2,18},{10... | collective-permute-start | bytes 393224 | tf_op jit(solution)/shard_map/ppermute | solution.py:174
  17.6 5.9 %collective-permute-start.3 = (bf16[256,256]{1,0:T(8,128)(2,1)S(1)}, bf16[256,256]{1,0:T(8,128)(2,1)S(1)}, u32[]{:S(2)}, u32[]{:S(2)}) collective-permute-start(bf16[256,256]{1,0:T(8,128)(2,1)S(1)} %collective-permute-done.rest_0_), channel_id=1, source_target_pairs={{0,24},{8,16},{16,8},{24,0},{1,25},{9,17},{17,9},{25,1},{2,26},{10... | collective-permute-start | bytes 393224 | tf_op jit(solution)/shard_map/ppermute | solution.py:174
  28.4 2.0 %collective-permute-start.5 = (f32[512,256]{1,0:T(8,128)S(1)}, f32[512,256]{1,0:T(8,128)S(1)}, u32[]{:S(2)}, u32[]{:S(2)}) collective-permute-start(f32[512,256]{1,0:T(8,128)S(1)} %get-tuple-element.16), channel_id=1, source_target_pairs={{0,1},{1,0},{2,3},{3,2},{4,5},{5,4},{6,7},{7,6},{8,9},{9,8},{10,11... | collective-permute-start | bytes 1572872 | tf_op jit(solution)/shard_map/ppermute | solution.py:249
  30.4 6.4 %collective-permute-start.6 = (f32[128,256]{1,0:T(8,128)S(1)}, f32[128,256]{1,0:T(8,128)S(1)}, u32[]{:S(2)}, u32[]{:S(2)}) collective-permute-start(f32[128,256]{1,0:T(8,128)S(1)} %get-tuple-element.18), channel_id=1, source_target_pairs={{0,8},{8,0},{16,24},{24,16},{1,9},{9,1},{17,25},{25,17},{2,10},{10... | collective-permute-start | bytes 393224 | tf_op jit(solution)/shard_map/ppermute | solution.py:262
  31.3 8.1 %collective-permute-start.7 = (f32[128,256]{1,0:T(8,128)S(1)}, f32[128,256]{1,0:T(8,128)S(1)}, u32[]{:S(2)}, u32[]{:S(2)}) collective-permute-start(f32[128,256]{1,0:T(8,128)S(1)} %get-tuple-element.19), channel_id=1, source_target_pairs={{0,16},{8,24},{16,0},{24,8},{1,17},{9,25},{17,1},{25,9},{2,18},{10... | collective-permute-start | bytes 393224 | tf_op jit(solution)/shard_map/ppermute | solution.py:262
  32.6 6.7 %collective-permute-start.8 = (f32[128,256]{1,0:T(8,128)S(1)}, f32[128,256]{1,0:T(8,128)S(1)}, u32[]{:S(2)}, u32[]{:S(2)}) collective-permute-start(f32[128,256]{1,0:T(8,128)S(1)} %get-tuple-element.20), channel_id=1, source_target_pairs={{0,24},{8,16},{16,8},{24,0},{1,25},{9,17},{17,9},{25,1},{2,26},{10... | collective-permute-start | bytes 393224 | tf_op jit(solution)/shard_map/ppermute | solution.py:262
  39.4 1.4 %collective-permute-start.9 = (f32[128,256]{1,0:T(8,128)S(1)}, f32[128,256]{1,0:T(8,128)S(1)}, u32[]{:S(2)}, u32[]{:S(2)}) collective-permute-start(f32[128,256]{1,0:T(8,128)S(1)} %add_multiply_fusion), channel_id=1, source_target_pairs={{0,1},{1,0},{2,3},{3,2},{4,5},{5,4},{6,7},{7,6},{8,9},{9,8},{10,11... | collective-permute-start | bytes 393224 | tf_op jit(solution)/shard_map/ppermute | solution.py:265

commit v3 on v2

--- a/solution.py
+++ b/solution.py
@@ -15,6 +15,10 @@
 HBM = pl.BlockSpec(memory_space=pltpu.HBM)
 
 
+SCALED_TOP = 14
+EXPONENT_ROWS = 16
+
+
 def exchange_pairs(distance, size):
     return [(i, i ^ distance) for i in range(size)]
 
@@ -23,11 +27,16 @@
     return pltpu.with_memory_space_constraint(x, pltpu.HBM)
 
 
+def slot_product(block, coef):
+    aux_total, width, _ = block.shape
+    product = jnp.dot(
+        block.reshape(aux_total * width, width), coef, preferred_element_type=jnp.float32
+    )
+    return product.reshape(aux_total, width, coef.shape[1])
+
+
 def add_slot(table, i, ints_ref, coef, acc_ref):
-    aux_total, _, _, width, _ = ints_ref.shape
-    left = ints_ref[:, 0, table[i]].reshape(aux_total * width, width)
-    product = jnp.dot(left, coef, preferred_element_type=jnp.float32)
-    acc_ref[...] += product.reshape(acc_ref.shape)
+    acc_ref[...] += slot_product(ints_ref[:, 0, table[i]], coef)
 
 
 def head_kernel(piece, t, coef_hbm, out_ref, sem):
@@ -40,13 +49,12 @@
     copy.wait()
 
 
-def own_kernel(counts, lists_hbm, ints_ref, coef_hbm, acc_ref, table, coef, lists, sems):
-    slot_total = ints_ref.shape[2]
+def first_kernel(counts, lists_hbm, ints_hbm, coef, acc_ref, table, lists, buffer, sems):
+    slot_total = ints_hbm.shape[2]
     lists_copy = pltpu.make_async_copy(lists_hbm, lists, sems.at[0])
+    slot_copy = pltpu.make_async_copy(ints_hbm.at[:, 0, 0], buffer, sems.at[1])
     lists_copy.start()
-    coef_copy = pltpu.make_async_copy(coef_hbm, coef, sems.at[1])
-    coef_copy.start()
-    acc_ref[...] = jnp.zeros_like(acc_ref)
+    slot_copy.start()
     lists_copy.wait()
     me = lax.axis_index("blk")
     live = counts[0]
@@ -58,19 +66,16 @@
             table[slot_total + 1 + found] = away
             found = found + ((slot < live) & (away >= lo) & (away < hi)).astype(jnp.int32)
         table[2 * slot_total + 2 + step] = found
-    coef_copy.wait()
-
-    @pl.loop(0, table[2 * slot_total + 2])
+    slot_copy.wait()
+    acc_ref[...] = slot_product(buffer[...], coef[...])
+
+
+def near_kernel(distance, table, ints_ref, coef_ref, _acc, acc_ref):
+    ends = 2 * ints_ref.shape[2] + 2
+
+    @pl.loop(table[ends + distance - 1] if distance else 1, table[ends + distance])
     def _(i):
-        add_slot(table, i, ints_ref, coef[...], acc_ref)
-
-
-def next_kernel(table, ints_ref, next_ref, _acc, acc_ref):
-    slot_total = ints_ref.shape[2]
-
-    @pl.loop(table[2 * slot_total + 2], table[2 * slot_total + 3])
-    def _(i):
-        add_slot(table, i, ints_ref, next_ref[...], acc_ref)
+        add_slot(table, i, ints_ref, coef_ref[...], acc_ref)
 
 
 def add_far(distances, complete_after, table, ints_ref, chunks, coef, acc_ref):
@@ -131,7 +136,18 @@
         total = terms[0][rows, :]
         for term in terms[1:]:
             total = total + term[rows, :]
-        outs[k][...] = total
+        if k == 0:
+            outs[k][...] = total
+            continue
+        peak = jnp.max(jnp.abs(total), axis=0, keepdims=True)
+        exponent = jnp.ceil(jnp.log(jnp.maximum(peak, 2.0**-100)) * (1 / math.log(2.0)))
+        outs[k][:depth, :] = total * jnp.exp2(SCALED_TOP - exponent)
+        outs[k][depth:, :] = jnp.broadcast_to(exponent, (EXPONENT_ROWS, total.shape[1]))
+
+
+def unscaled(block, depth):
+    block = block.astype(jnp.float32)
+    return block[:depth] * jnp.exp2(block[depth : depth + 1] - SCALED_TOP)
 
 
 def per_device(integrals, orbitals, pair_lists, pair_counts):
@@ -164,15 +180,12 @@
             out_specs=VMEM,
             scratch_shapes=[pltpu.SemaphoreType.DMA],
             compiler_params=pltpu.CompilerParams(vmem_limit_bytes=1 << 20),
-            cost_estimate=cost(8 * slot_total),
+            cost_estimate=cost(4 * slot_total),
             name="head",
         )(in_hbm(orbitals))
         parts.append(lax.ppermute(sent, ("aux", "blk"), pairs))
     next_block = lax.ppermute(orbitals, "blk", exchange_pairs(1, blk_size))
     chunk = parts[0] if len(parts) == 1 else jnp.concatenate(parts, 0)
-    chunks = [chunk] + [
-        lax.ppermute(chunk, "aux", exchange_pairs(k, aux_size)) for k in range(1, aux_size)
-    ]
 
     acc_shape = jax.ShapeDtypeStruct((aux_total, width, columns), jnp.float32)
     table_shape = jax.ShapeDtypeStruct((2 * slot_total + 5,), jnp.int32)
@@ -180,29 +193,37 @@
     ints = integrals
 
     acc, table = pl.pallas_call(
-        own_kernel,
+        first_kernel,
         out_shape=(acc_shape, table_shape),
-        in_specs=[SMEM, HBM, VMEM, HBM],
+        in_specs=[SMEM, HBM, HBM, VMEM],
         out_specs=(VMEM, SMEM),
         scratch_shapes=[
-            pltpu.VMEM((width, columns), jnp.bfloat16),
             pltpu.SMEM(pair_lists.shape, jnp.int32),
+            pltpu.VMEM((aux_total, width, width), jnp.bfloat16),
             pltpu.SemaphoreType.DMA((2,)),
         ],
-        compiler_params=small,
-        cost_estimate=cost(3),
-        name="own",
-    )(pair_counts, in_hbm(pair_lists), ints, in_hbm(orbitals))
-    acc = pl.pallas_call(
-        next_kernel,
-        out_shape=acc_shape,
-        in_specs=[SMEM, VMEM, VMEM, VMEM],
-        out_specs=VMEM,
-        input_output_aliases={3: 0},
-        compiler_params=small,
-        cost_estimate=cost(3),
-        name="next",
-    )(table, ints, next_block, acc)
+        compiler_params=pltpu.CompilerParams(vmem_limit_bytes=(6 << 20) + slot_bytes),
+        cost_estimate=cost(1),
+        name="first",
+    )(pair_counts, in_hbm(pair_lists), in_hbm(integrals), orbitals)
+
+    def near(distance, coef, acc):
+        return pl.pallas_call(
+            functools.partial(near_kernel, distance),
+            out_shape=acc_shape,
+            in_specs=[SMEM, VMEM, VMEM, VMEM],
+            out_specs=VMEM,
+            input_output_aliases={3: 0},
+            compiler_params=small,
+            cost_estimate=cost(2),
+        )(table, ints, coef, acc)
+
+    acc = near(0, orbitals, acc)
+    chunk, acc = lax.optimization_barrier((chunk, acc))
+    chunks = [chunk] + [
+        lax.ppermute(chunk, "aux", exchange_pairs(k, aux_size)) for k in range(1, aux_size)
+    ]
+    acc = near(1, next_block, acc)
 
     share = width // occ_size
     piece_shape = jax.ShapeDtypeStruct((width, share), jnp.float32)
@@ -251,7 +272,8 @@
     rows = width // aux_size
     mine = pl.pallas_call(
         split_kernel,
-        out_shape=[jax.ShapeDtypeStruct((rows, share), jnp.float32)] * aux_size,
+        out_shape=[jax.ShapeDtypeStruct((rows, share), jnp.float32)]
+        + [jax.ShapeDtypeStruct((rows + EXPONENT_ROWS, share), jnp.float32)] * (aux_size - 1),
         in_specs=[VMEM] * occ_size,
         out_specs=[VMEM] * aux_size,
         compiler_params=pltpu.CompilerParams(vmem_limit_bytes=8 << 20),
@@ -259,7 +281,8 @@
     )(*terms)
     total = mine[0]
     for k in range(1, aux_size):
-        total = total + lax.ppermute(mine[k], "aux", exchange_pairs(k, aux_size))
+        sent = mine[k].astype(jnp.float16)
+        total = total + unscaled(lax.ppermute(sent, "aux", exchange_pairs(k, aux_size)), rows)
     total = total / (columns * occ_size)
     shares = [total] + [
         lax.ppermute(total, "occ", exchange_pairs(k, occ_size)) for k in range(1, occ_size)

time: 41.7 us -> 40.8 us (0.978)
  local copies, waits for them, and re-layouts: 2.52 us -> 0.19 us
  Pallas kernels: 12.9 us -> 14.8 us
  waiting for transfers between devices: 10.5 us -> 8.96 us
  starting transfers between devices: 13.3 us -> 14.2 us
    unnamed x2 -> x14, local copies, waits for them, and re-layouts: 2.52 us -> 0.19 us
    pallas_call x2 -> x3, Pallas kernels: 4.23 us -> 5.73 us  [the longest x1 3.14 us: per_device(): pl.pallas_call(first_kernel, out_shape=(acc_shape, table_shape), in_specs...]
    ppermute x3, waiting for transfers between devices: 5.36 us -> 3.94 us  [per_device(): lax.ppermute(sent, 'aux', exchange_pairs(k, aux_size))]
    ppermute x3, starting transfers between devices: 3.89 us -> 4.63 us  [per_device(): lax.ppermute(chunk, 'aux', exchange_pairs(k, aux_size))]
  transfers between devices with their start and end apart: 10 -> 10, of which waited for: 7 -> 7; matrix products, arithmetic and copies ran while one was open for 0% -> 0% of each run, Pallas kernels for 19% -> 24%
where the time goes in v3:
time: 40.8 us; the launch traced here: 40.6 us
  Pallas kernels  14.8 us (36%)
  starting transfers between devices  14.2 us (35%)
  waiting for transfers between devices  8.96 us (22%)
  between operations  1.67 us (4%)
  other arithmetic  0.88 us (2%)
    pallas_call x1, Pallas kernels, per_device(): pl.pallas_call(functools.partial(last_kernel, (2, aux_size - 1), needed,...  5.13 us
    ppermute x3, starting transfers between devices, per_device(): lax.ppermute(chunk, 'aux', exchange_pairs(k, aux_size))  4.63 us
    ppermute x3, waiting for transfers between devices, per_device(): lax.ppermute(sent, 'aux', exchange_pairs(k, aux_size))  3.94 us
    ppermute x3, starting transfers between devices, per_device(): lax.ppermute(sent, 'aux', exchange_pairs(k, aux_size))  3.68 us
    pallas_call x1, Pallas kernels, per_device(): pl.pallas_call(first_kernel, out_shape=(acc_shape, table_shape), in_specs...  3.14 us
    ppermute x1, starting transfers between devices, per_device(): next_block = lax.ppermute(orbitals, 'blk', exchange_pairs(1, blk_size))  3.05 us
    ppermute x1, starting transfers between devices, per_device(): parts.append(lax.ppermute(sent, ('aux', 'blk'), pairs))  2.65 us
    pallas_call x2, Pallas kernels, near(): pl.pallas_call(functools.partial(near_kernel, distance), out_shape=acc_sh...  2.59 us
  transfers between devices with their start and end apart: 10, of which 7 were waited for; matrix products, arithmetic and copies ran while one was open for 0% of the time, Pallas kernels for 24%

profile of v3, /device:TPU:0, one launch (start us, length us, event | category | flops | bytes accessed | tf_op | source)
XLA Modules:
  0.0 40.6 jit_solution(3825194383774019942)
XLA Ops:
  0.0 3.1 %collective-permute-start.4 = (bf16[512,256]{1,0:T(8,128)(2,1)}, bf16[512,256]{1,0:T(8,128)(2,1)S(1)}, u32[]{:S(2)}, u32[]{:S(2)}) collective-permute-start(bf16[512,256]{1,0:T(8,128)(2,1)} %coef_ref.1), channel_id=1, source_target_pairs={{0,2},{2,0},{4,6},{6,4},{1,3},{3,1},{5,7},{7,5},{8,10},{10,8},{12,... | collective-permute-start | bytes 786440 | tf_op jit(solution)/shard_map/ppermute | solution.py:187
  3.1 0.0 slice-start.4
  3.1 1.1 %head.1 = bf16[256,256]{1,0:T(8,128)(2,1)S(1)} custom-call(bf16[512,256]{1,0:T(8,128)(2,1)} %coef_ref.1), custom_call_target="tpu_custom_call" | custom-call | flops 23622320128 | bytes 92274688 | tf_op jit(solution)/shard_map/head/pallas_call | solution.py:176
  4.2 2.7 %collective-permute-start = (bf16[256,256]{1,0:T(8,128)(2,1)S(1)}, bf16[256,256]{1,0:T(8,128)(2,1)S(1)}, u32[]{:S(2)}, u32[]{:S(2)}) collective-permute-start(bf16[256,256]{1,0:T(8,128)(2,1)S(1)} %head.1), channel_id=1, source_target_pairs={{0,4},{2,6},{4,0},{6,2},{8,12},{10,14},{12,8},{14,10},{16,22},{18,... | collective-permute-start | bytes 393224 | tf_op jit(solution)/shard_map/ppermute | solution.py:186
  8.3 0.0 slice-start.5
  8.3 3.1 %first.1 = (f32[4,512,256]{2,1,0:T(8,128)S(1)}, s32[27]{0:T(128)S(1)}) custom-call(s32[1]{0:T(128)S(6)} %copy.13.counts, s32[1,11]{1,0:T(1,128)} %lists_hbm.1, bf16[4,1,11,512,512]{4,3,2,1,0:T(8,128)(2,1)} %ints_ref.7, bf16[512,256]{1,0:T(8,128)(2,1)S(1)} %copy-done), custom_call_target="tpu_custom_call" | custom-call | flops 536870912 | bytes 2097152 | tf_op jit(solution)/shard_map/first/pallas_call | solution.py:195
  11.5 0.2 slice-done.5
  11.6 1.3 %shard_map.46._acc = f32[4,512,256]{2,1,0:T(8,128)S(1)} custom-call(s32[27]{0:T(128)S(1)} %get-tuple-element.15.table, bf16[4,1,11,512,512]{4,3,2,1,0:T(8,128)(2,1)S(1)} %bitcast.6, bf16[512,256]{1,0:T(8,128)(2,1)S(1)} %copy-done, f32[4,512,256]{2,1,0:T(8,128)S(1)} %get-tuple-element.16._acc), custom_call_target="tpu_custom_call", output_to_operand_aliasing={{}: (3, {})} | custom-call | flops 1073741824 | bytes 4194304 | tf_op jit(solution)/shard_map/pallas_call | solution.py:211
  12.9 0.0 collective-permute-done.rest_0_
  13.0 1.6 %collective-permute-start.1 = (bf16[256,256]{1,0:T(8,128)(2,1)S(1)}, bf16[256,256]{1,0:T(8,128)(2,1)S(1)}, u32[]{:S(2)}, u32[]{:S(2)}) collective-permute-start(bf16[256,256]{1,0:T(8,128)(2,1)S(1)} %collective-permute-done.rest_0_), channel_id=1, source_target_pairs={{0,8},{8,0},{16,24},{24,16},{1,9},{9,1},{17,25},{25,17},{2,10},{10... | collective-permute-start | bytes 393224 | tf_op jit(solution)/shard_map/ppermute | solution.py:224
  14.5 3.1 %collective-permute-start.2 = (bf16[256,256]{1,0:T(8,128)(2,1)S(1)}, bf16[256,256]{1,0:T(8,128)(2,1)S(1)}, u32[]{:S(2)}, u32[]{:S(2)}) collective-permute-start(bf16[256,256]{1,0:T(8,128)(2,1)S(1)} %collective-permute-done.rest_0_), channel_id=1, source_target_pairs={{0,16},{8,24},{16,0},{24,8},{1,17},{9,25},{17,1},{25,9},{2,18},{10... | collective-permute-start | bytes 393224 | tf_op jit(solution)/shard_map/ppermute | solution.py:224
  17.6 0.0 collective-permute-start.3
  17.6 0.0 collective-permute-done.4.coef_ref
  17.6 1.3 %shard_map.47.rest_2_ = f32[4,512,256]{2,1,0:T(8,128)S(1)} custom-call(s32[27]{0:T(128)S(1)} %get-tuple-element.15.table, bf16[4,1,11,512,512]{4,3,2,1,0:T(8,128)(2,1)S(1)} %bitcast.6, bf16[512,256]{1,0:T(8,128)(2,1)S(1)} %collective-permute-done.4.coef_ref, f32[4,512,256]{2,1,0:T(8,128)S(1)} %shard_map.46._acc), custom_call_target="tpu_custom_call", output_to_operand_aliasing={{}: (3, {})} | custom-call | flops 1073741824 | bytes 4194304 | tf_op jit(solution)/shard_map/pallas_call | solution.py:211
  18.9 0.0 collective-permute-done.1.rest_1_
  18.9 2.3 %far.1.rest_4_ = f32[4,512,256]{2,1,0:T(8,128)S(1)} custom-call(s32[27]{0:T(128)S(1)} %get-tuple-element.15.table, bf16[4,1,11,512,512]{4,3,2,1,0:T(8,128)(2,1)S(1)} %bitcast.6, bf16[256,256]{1,0:T(8,128)(2,1)S(1)} %collective-permute-done.rest_0_, bf16[256,256]{1,0:T(8,128)(2,1)S(1)} %collective-permute-done.1.rest_1_, ...), custom_call_target="tpu_custom_call", output_to_operand_aliasing={{}: (4, {})} | custom-call | flops 1610612736 | bytes 6291456 | tf_op jit(solution)/shard_map/far/pallas_call | solution.py:236
  21.2 0.8 %collective-permute-done.2.rest_2_ = bf16[256,256]{1,0:T(8,128)(2,1)S(1)} collective-permute-done((bf16[256,256]{1,0:T(8,128)(2,1)S(1)}, bf16[256,256]{1,0:T(8,128)(2,1)S(1)}, u32[]{:S(2)}, u32[]{:S(2)}) %collective-permute-start.2) | collective-permute-done | bytes 131104 | tf_op jit(solution)/shard_map/ppermute | solution.py:224
  22.0 1.4 %collective-permute-done.3.rest_3_ = bf16[256,256]{1,0:T(8,128)(2,1)S(1)} collective-permute-done((bf16[256,256]{1,0:T(8,128)(2,1)S(1)}, bf16[256,256]{1,0:T(8,128)(2,1)S(1)}, u32[]{:S(2)}, u32[]{:S(2)}) %collective-permute-start.3) | collective-permute-done | bytes 131104 | tf_op jit(solution)/shard_map/ppermute | solution.py:224
  23.4 5.1 %last.1 = (f32[4,512,256]{2,1,0:T(8,128)S(1)}, bf16[512,1024]{1,0:T(8,128)(2,1)S(1)}, f32[512,256]{1,0:T(8,128)S(1)}) custom-call(s32[27]{0:T(128)S(1)} %get-tuple-element.15.table, bf16[4,1,11,512,512]{4,3,2,1,0:T(8,128)(2,1)S(1)} %bitcast.6, bf16[256,256]{1,0:T(8,128)(2,1)S(1)} %collective-permute-done.rest_0_, ...), custom_call_target="tpu_custom_call", output_to_operand_aliasing={{0}: (6, {})} | custom-call | flops 1610612736 | bytes 6291456 | tf_op jit(solution)/shard_map/last/pallas_call | solution.py:248
  28.6 0.1 collective-permute-start.5
  28.7 0.5 %kept.1.refs_0_ = f32[512,256]{1,0:T(8,128)S(1)} custom-call(bf16[512,1024]{1,0:T(8,128)(2,1)S(1)} %get-tuple-element.19.halves), custom_call_target="tpu_custom_call" | custom-call | flops 536870912 | bytes 2097152 | tf_op jit(solution)/shard_map/kept/pallas_call | solution.py:259
  29.2 1.4 %collective-permute-done.5.refs_1_ = f32[512,256]{1,0:T(8,128)S(1)} collective-permute-done((f32[512,256]{1,0:T(8,128)S(1)}, f32[512,256]{1,0:T(8,128)S(1)}, u32[]{:S(2)}, u32[]{:S(2)}) %collective-permute-start.5) | collective-permute-done | bytes 524320 | tf_op jit(solution)/shard_map/ppermute | solution.py:270
  30.6 0.1 split.1
  30.7 0.9 %collective-permute-start.6 = (f16[144,256]{1,0:T(8,128)(2,1)S(1)}, f16[144,256]{1,0:T(8,128)(2,1)S(1)}, u32[]{:S(2)}, u32[]{:S(2)}) collective-permute-start(f16[144,256]{1,0:T(8,128)(2,1)S(1)} %convert_element_type.18), channel_id=1, source_target_pairs={{0,8},{8,0},{16,24},{24,16},{1,9},{9,1},{17,25},{25,17},{2,10},{10... | collective-permute-start | bytes 221192 | tf_op jit(solution)/shard_map/ppermute | solution.py:285
  31.6 1.5 %collective-permute-start.7 = (f16[144,256]{1,0:T(8,128)(2,1)S(1)}, f16[144,256]{1,0:T(8,128)(2,1)S(1)}, u32[]{:S(2)}, u32[]{:S(2)}) collective-permute-start(f16[144,256]{1,0:T(8,128)(2,1)S(1)} %convert_element_type.20), channel_id=1, source_target_pairs={{0,16},{8,24},{16,0},{24,8},{1,17},{9,25},{17,1},{25,9},{2,18},{10... | collective-permute-start | bytes 221192 | tf_op jit(solution)/shard_map/ppermute | solution.py:285
  33.1 1.3 %collective-permute-start.8 = (f16[144,256]{1,0:T(8,128)(2,1)S(1)}, f16[144,256]{1,0:T(8,128)(2,1)S(1)}, u32[]{:S(2)}, u32[]{:S(2)}) collective-permute-start(f16[144,256]{1,0:T(8,128)(2,1)S(1)} %convert_element_type.22), channel_id=1, source_target_pairs={{0,24},{8,16},{16,8},{24,0},{1,25},{9,17},{17,9},{25,1},{2,26},{10... | collective-permute-start | bytes 221192 | tf_op jit(solution)/shard_map/ppermute | solution.py:285
  34.4 0.7 %collective-permute-done.6 = f16[144,256]{1,0:T(8,128)(2,1)S(1)} collective-permute-done((f16[144,256]{1,0:T(8,128)(2,1)S(1)}, f16[144,256]{1,0:T(8,128)(2,1)S(1)}, u32[]{:S(2)}, u32[]{:S(2)}) %collective-permute-start.6) | collective-permute-done | bytes 73760 | tf_op jit(solution)/shard_map/ppermute | solution.py:285
  35.1 0.8 %collective-permute-done.7 = f16[144,256]{1,0:T(8,128)(2,1)S(1)} collective-permute-done((f16[144,256]{1,0:T(8,128)(2,1)S(1)}, f16[144,256]{1,0:T(8,128)(2,1)S(1)}, u32[]{:S(2)}, u32[]{:S(2)}) %collective-permute-start.7) | collective-permute-done | bytes 73760 | tf_op jit(solution)/shard_map/ppermute | solution.py:285
  36.0 2.4 %collective-permute-done.8 = f16[144,256]{1,0:T(8,128)(2,1)S(1)} collective-permute-done((f16[144,256]{1,0:T(8,128)(2,1)S(1)}, f16[144,256]{1,0:T(8,128)(2,1)S(1)}, u32[]{:S(2)}, u32[]{:S(2)}) %collective-permute-start.8) | collective-permute-done | bytes 73760 | tf_op jit(solution)/shard_map/ppermute | solution.py:285
  38.5 0.1 collective-permute-start.9
  38.6 1.3 %collective-permute-done.9 = f32[128,256]{1,0:T(8,128)S(1)} collective-permute-done((f32[128,256]{1,0:T(8,128)S(1)}, f32[128,256]{1,0:T(8,128)S(1)}, u32[]{:S(2)}, u32[]{:S(2)}) %collective-permute-start.9) | collective-permute-done | bytes 131104 | tf_op jit(solution)/shard_map/ppermute | solution.py:288
  39.9 0.7 %maximum_bitcast_fusion = f32[1,128,512]{2,1,0:T(8,128)} fusion(f32[128,256]{1,0:T(8,128)S(1)} %get-tuple-element.26, f32[128,256]{1,0:T(8,128)S(1)} %get-tuple-element.25), kind=kLoop, calls=%fused_computation | loop fusion | flops 65536 | bytes 524288 | tf_op jit(solution)/shard_map/broadcast_in_dim | solution.py:296
  (23 shorter events, 0.2 us)
Async XLA Ops:
  0.0 8.3 %copy-start = (bf16[512,256]{1,0:T(8,128)(2,1)S(1)}, bf16[512,256]{1,0:T(8,128)(2,1)}, u32[]{:S(2)}) copy-start(bf16[512,256]{1,0:T(8,128)(2,1)} %coef_ref.1) | copy-start | bytes 786436
  0.0 17.6 %collective-permute-start.4 = (bf16[512,256]{1,0:T(8,128)(2,1)}, bf16[512,256]{1,0:T(8,128)(2,1)S(1)}, u32[]{:S(2)}, u32[]{:S(2)}) collective-permute-start(bf16[512,256]{1,0:T(8,128)(2,1)} %coef_ref.1), channel_id=1, source_target_pairs={{0,2},{2,0},{4,6},{6,4},{1,3},{3,1},{5,7},{7,5},{8,10},{10,8},{12,... | collective-permute-start | bytes 786440 | tf_op jit(solution)/shard_map/ppermute | solution.py:187
  3.1 8.4 %slice-start = ((s8[23068672]{0:T(1024)(128)(4,1)}), s8[4194304]{0:T(1024)(128)(4,1)S(1)}, s32[]{:S(2)}) async-start(s8[23068672]{0:T(1024)(128)(4,1)} %bitcast.5), calls=%async_computation | async-start | bytes 8388608
  3.1 8.4 %slice-start.1 = ((s8[23068672]{0:T(1024)(128)(4,1)}), s8[4194304]{0:T(1024)(128)(4,1)S(1)}, s32[]{:S(2)}) async-start(s8[23068672]{0:T(1024)(128)(4,1)} %bitcast.5), calls=%async_computation.1 | async-start | bytes 8388608
  3.1 8.4 %slice-start.2 = ((s8[23068672]{0:T(1024)(128)(4,1)}), s8[4194304]{0:T(1024)(128)(4,1)S(1)}, s32[]{:S(2)}) async-start(s8[23068672]{0:T(1024)(128)(4,1)} %bitcast.5), calls=%async_computation.2 | async-start | bytes 8388608
  3.1 8.4 %slice-start.3 = ((s8[23068672]{0:T(1024)(128)(4,1)}), s8[4194304]{0:T(1024)(128)(4,1)S(1)}, s32[]{:S(2)}) async-start(s8[23068672]{0:T(1024)(128)(4,1)} %bitcast.5), calls=%async_computation.3 | async-start | bytes 8388608
  3.1 8.4 %slice-start.4 = ((s8[23068672]{0:T(1024)(128)(4,1)}), s8[4194304]{0:T(1024)(128)(4,1)S(1)}, s32[]{:S(2)}) async-start(s8[23068672]{0:T(1024)(128)(4,1)} %bitcast.5), calls=%async_computation.4 | async-start | bytes 8388608
  4.2 8.8 %collective-permute-start = (bf16[256,256]{1,0:T(8,128)(2,1)S(1)}, bf16[256,256]{1,0:T(8,128)(2,1)S(1)}, u32[]{:S(2)}, u32[]{:S(2)}) collective-permute-start(bf16[256,256]{1,0:T(8,128)(2,1)S(1)} %head.1), channel_id=1, source_target_pairs={{0,4},{2,6},{4,0},{6,2},{8,12},{10,14},{12,8},{14,10},{16,22},{18,... | collective-permute-start | bytes 393224 | tf_op jit(solution)/shard_map/ppermute | solution.py:186
  8.3 3.4 %slice-start.5 = ((s8[23068672]{0:T(1024)(128)(4,1)}), s8[2097152]{0:T(1024)(128)(4,1)S(1)}, s32[]{:S(2)}) async-start(s8[23068672]{0:T(1024)(128)(4,1)} %bitcast.5), calls=%async_computation.5 | async-start | bytes 4194304
  13.0 5.9 %collective-permute-start.1 = (bf16[256,256]{1,0:T(8,128)(2,1)S(1)}, bf16[256,256]{1,0:T(8,128)(2,1)S(1)}, u32[]{:S(2)}, u32[]{:S(2)}) collective-permute-start(bf16[256,256]{1,0:T(8,128)(2,1)S(1)} %collective-permute-done.rest_0_), channel_id=1, source_target_pairs={{0,8},{8,0},{16,24},{24,16},{1,9},{9,1},{17,25},{25,17},{2,10},{10... | collective-permute-start | bytes 393224 | tf_op jit(solution)/shard_map/ppermute | solution.py:224
  14.5 7.5 %collective-permute-start.2 = (bf16[256,256]{1,0:T(8,128)(2,1)S(1)}, bf16[256,256]{1,0:T(8,128)(2,1)S(1)}, u32[]{:S(2)}, u32[]{:S(2)}) collective-permute-start(bf16[256,256]{1,0:T(8,128)(2,1)S(1)} %collective-permute-done.rest_0_), channel_id=1, source_target_pairs={{0,16},{8,24},{16,0},{24,8},{1,17},{9,25},{17,1},{25,9},{2,18},{10... | collective-permute-start | bytes 393224 | tf_op jit(solution)/shard_map/ppermute | solution.py:224
  17.6 5.9 %collective-permute-start.3 = (bf16[256,256]{1,0:T(8,128)(2,1)S(1)}, bf16[256,256]{1,0:T(8,128)(2,1)S(1)}, u32[]{:S(2)}, u32[]{:S(2)}) collective-permute-start(bf16[256,256]{1,0:T(8,128)(2,1)S(1)} %collective-permute-done.rest_0_), channel_id=1, source_target_pairs={{0,24},{8,16},{16,8},{24,0},{1,25},{9,17},{17,9},{25,1},{2,26},{10... | collective-permute-start | bytes 393224 | tf_op jit(solution)/shard_map/ppermute | solution.py:224
  28.6 2.0 %collective-permute-start.5 = (f32[512,256]{1,0:T(8,128)S(1)}, f32[512,256]{1,0:T(8,128)S(1)}, u32[]{:S(2)}, u32[]{:S(2)}) collective-permute-start(f32[512,256]{1,0:T(8,128)S(1)} %get-tuple-element.20), channel_id=1, source_target_pairs={{0,1},{1,0},{2,3},{3,2},{4,5},{5,4},{6,7},{7,6},{8,9},{9,8},{10,11... | collective-permute-start | bytes 1572872 | tf_op jit(solution)/shard_map/ppermute | solution.py:270
  30.7 4.4 %collective-permute-start.6 = (f16[144,256]{1,0:T(8,128)(2,1)S(1)}, f16[144,256]{1,0:T(8,128)(2,1)S(1)}, u32[]{:S(2)}, u32[]{:S(2)}) collective-permute-start(f16[144,256]{1,0:T(8,128)(2,1)S(1)} %convert_element_type.18), channel_id=1, source_target_pairs={{0,8},{8,0},{16,24},{24,16},{1,9},{9,1},{17,25},{25,17},{2,10},{10... | collective-permute-start | bytes 221192 | tf_op jit(solution)/shard_map/ppermute | solution.py:285
  31.6 4.4 %collective-permute-start.7 = (f16[144,256]{1,0:T(8,128)(2,1)S(1)}, f16[144,256]{1,0:T(8,128)(2,1)S(1)}, u32[]{:S(2)}, u32[]{:S(2)}) collective-permute-start(f16[144,256]{1,0:T(8,128)(2,1)S(1)} %convert_element_type.20), channel_id=1, source_target_pairs={{0,16},{8,24},{16,0},{24,8},{1,17},{9,25},{17,1},{25,9},{2,18},{10... | collective-permute-start | bytes 221192 | tf_op jit(solution)/shard_map/ppermute | solution.py:285
  33.1 5.3 %collective-permute-start.8 = (f16[144,256]{1,0:T(8,128)(2,1)S(1)}, f16[144,256]{1,0:T(8,128)(2,1)S(1)}, u32[]{:S(2)}, u32[]{:S(2)}) collective-permute-start(f16[144,256]{1,0:T(8,128)(2,1)S(1)} %convert_element_type.22), channel_id=1, source_target_pairs={{0,24},{8,16},{16,8},{24,0},{1,25},{9,17},{17,9},{25,1},{2,26},{10... | collective-permute-start | bytes 221192 | tf_op jit(solution)/shard_map/ppermute | solution.py:285
  38.5 1.4 %collective-permute-start.9 = (f32[128,256]{1,0:T(8,128)S(1)}, f32[128,256]{1,0:T(8,128)S(1)}, u32[]{:S(2)}, u32[]{:S(2)}) collective-permute-start(f32[128,256]{1,0:T(8,128)S(1)} %fusion.1), channel_id=1, source_target_pairs={{0,1},{1,0},{2,3},{3,2},{4,5},{5,4},{6,7},{7,6},{8,9},{9,8},{10,11... | collective-permute-start | bytes 393224 | tf_op jit(solution)/shard_map/ppermute | solution.py:288

commit v4 on v3

--- a/solution.py
+++ b/solution.py
@@ -35,8 +35,30 @@
     return product.reshape(aux_total, width, coef.shape[1])
 
 
-def add_slot(table, i, ints_ref, coef, acc_ref):
-    acc_ref[...] += slot_product(ints_ref[:, 0, table[i]], coef)
+def add_slots(table, group, ints_ref, coef_rows, acc_ref, fresh=False):
+    begin, end = group_bounds(table, group, ints_ref.shape[2])
+
+    def product(i):
+        return slot_product(ints_ref[:, 0, table[i]], coef_rows(i))
+
+    if fresh:
+        acc_ref[...] = product(0)
+        begin = 1
+    pairs = (end - begin) // 2
+
+    @pl.loop(0, pairs)
+    def _(pair):
+        i = begin + 2 * pair
+        acc_ref[...] += product(i) + product(i + 1)
+
+    @pl.when(begin + 2 * pairs < end)
+    def _():
+        acc_ref[...] += product(end - 1)
+
+
+def group_bounds(table, group, slot_total):
+    ends = 2 * slot_total + 2
+    return (table[ends + group - 1] if group else 0), table[ends + group]
 
 
 def head_kernel(piece, t, coef_hbm, out_ref, sem):
@@ -49,67 +71,59 @@
     copy.wait()
 
 
-def first_kernel(counts, lists_hbm, ints_hbm, coef, acc_ref, table, lists, buffer, sems):
-    slot_total = ints_hbm.shape[2]
-    lists_copy = pltpu.make_async_copy(lists_hbm, lists, sems.at[0])
-    slot_copy = pltpu.make_async_copy(ints_hbm.at[:, 0, 0], buffer, sems.at[1])
-    lists_copy.start()
-    slot_copy.start()
-    lists_copy.wait()
-    me = lax.axis_index("blk")
+def sort_kernel(far_depth, width, counts, lists_hbm, table, lists, sem):
+    slot_total = lists.shape[1]
+    copy = pltpu.make_async_copy(lists_hbm, lists, sem)
+    copy.start()
+    copy.wait()
+    me, my_aux = lax.axis_index("blk"), lax.axis_index("aux")
     live = counts[0]
+    piece = math.gcd(far_depth, width)
+    groups = []
+    for slot in range(slot_total):
+        away = lists[0, slot] ^ me
+        last = jnp.int32(0)
+        for part in range(width // piece):
+            last = jnp.maximum(last, lax.div((away - 2) * width + part * piece, far_depth) ^ my_aux)
+        far_group = jnp.where(last <= 1, 2, 3)
+        groups.append(jnp.where(slot < live, jnp.where(away < 2, away, far_group), 4))
     found = jnp.int32(0)
-    for step, (lo, hi) in enumerate(((0, 1), (1, 2), (2, 1 << 30))):
+    for group in range(4):
         for slot in range(slot_total):
-            away = lists[0, slot] ^ me
             table[found] = slot
-            table[slot_total + 1 + found] = away
-            found = found + ((slot < live) & (away >= lo) & (away < hi)).astype(jnp.int32)
-        table[2 * slot_total + 2 + step] = found
-    slot_copy.wait()
-    acc_ref[...] = slot_product(buffer[...], coef[...])
-
-
-def near_kernel(distance, table, ints_ref, coef_ref, _acc, acc_ref):
-    ends = 2 * ints_ref.shape[2] + 2
-
-    @pl.loop(table[ends + distance - 1] if distance else 1, table[ends + distance])
-    def _(i):
-        add_slot(table, i, ints_ref, coef_ref[...], acc_ref)
-
-
-def add_far(distances, complete_after, table, ints_ref, chunks, coef, acc_ref):
+            table[slot_total + 1 + found] = lists[0, slot] ^ me
+            found = found + (groups[slot] == group).astype(jnp.int32)
+        table[2 * slot_total + 2 + group] = found
+
+
+def near_kernel(group, table, ints_ref, coef_ref, *accs):
+    add_slots(table, group, ints_ref, lambda i: coef_ref[...], accs[-1], fresh=group == 0)
+
+
+def add_far(group, needed, table, ints_ref, chunks, coef, acc_ref):
     _, _, slot_total, width, _ = ints_ref.shape
     depth = chunks[0].shape[0]
-    piece = math.gcd(depth, width)
     me = lax.axis_index("aux")
-    for k, chunk in enumerate(chunks):
-        if k in complete_after:
-            rows = pl.ds(pl.multiple_of((me ^ k) * depth, depth), depth)
-            coef[rows, :] = chunk[...]
-
-    @pl.loop(table[2 * slot_total + 3], table[2 * slot_total + 4])
-    def _(i):
+    for k in needed:
+        rows = pl.ds(pl.multiple_of((me ^ k) * depth, depth), depth)
+        coef[rows, :] = chunks[k][...]
+
+    def coef_rows(i):
         start = (table[slot_total + 1 + i] - 2) * width
-        last = jnp.int32(0)
-        for part in range(width // piece):
-            last = jnp.maximum(last, ((start + part * piece) // depth) ^ me)
-
-        @pl.when((last >= distances[0]) & (last <= distances[-1]))
-        def _():
-            rows = pl.ds(pl.multiple_of(start, width), width)
-            add_slot(table, i, ints_ref, coef[rows, :], acc_ref)
-
-
-def far_kernel(distances, needed, table, ints_ref, *rest):
+        return coef[pl.ds(pl.multiple_of(start, width), width), :]
+
+    add_slots(table, group, ints_ref, coef_rows, acc_ref)
+
+
+def far_kernel(needed, table, ints_ref, *rest):
     *chunks, _, acc_ref, coef = rest
-    add_far(distances, needed, table, ints_ref, chunks, coef, acc_ref)
-
-
-def last_kernel(distances, needed, occ_size, table, ints_ref, *rest):
+    add_far(2, needed, table, ints_ref, chunks, coef, acc_ref)
+
+
+def last_kernel(needed, occ_size, table, ints_ref, *rest):
     *chunks, _, acc_ref, halves = rest[: -occ_size]
     pieces, coef = rest[-occ_size:-1], rest[-1]
-    add_far(distances, needed, table, ints_ref, chunks, coef, acc_ref)
+    add_far(3, needed, table, ints_ref, chunks, coef, acc_ref)
     columns = acc_ref.shape[2]
     for p in range(acc_ref.shape[0]):
         halves[:, p * columns : (p + 1) * columns] = acc_ref[p].astype(jnp.bfloat16)
@@ -188,37 +202,33 @@
     chunk = parts[0] if len(parts) == 1 else jnp.concatenate(parts, 0)
 
     acc_shape = jax.ShapeDtypeStruct((aux_total, width, columns), jnp.float32)
-    table_shape = jax.ShapeDtypeStruct((2 * slot_total + 5,), jnp.int32)
-    small = pltpu.CompilerParams(vmem_limit_bytes=8 << 20)
+    table_shape = jax.ShapeDtypeStruct((2 * slot_total + 6,), jnp.int32)
+    small = pltpu.CompilerParams(vmem_limit_bytes=10 << 20)
     ints = integrals
 
-    acc, table = pl.pallas_call(
-        first_kernel,
-        out_shape=(acc_shape, table_shape),
-        in_specs=[SMEM, HBM, HBM, VMEM],
-        out_specs=(VMEM, SMEM),
-        scratch_shapes=[
-            pltpu.SMEM(pair_lists.shape, jnp.int32),
-            pltpu.VMEM((aux_total, width, width), jnp.bfloat16),
-            pltpu.SemaphoreType.DMA((2,)),
-        ],
-        compiler_params=pltpu.CompilerParams(vmem_limit_bytes=(6 << 20) + slot_bytes),
+    table = pl.pallas_call(
+        functools.partial(sort_kernel, depth, width),
+        out_shape=table_shape,
+        in_specs=[SMEM, HBM],
+        out_specs=SMEM,
+        scratch_shapes=[pltpu.SMEM(pair_lists.shape, jnp.int32), pltpu.SemaphoreType.DMA],
+        compiler_params=pltpu.CompilerParams(vmem_limit_bytes=1 << 20),
         cost_estimate=cost(1),
-        name="first",
-    )(pair_counts, in_hbm(pair_lists), in_hbm(integrals), orbitals)
-
-    def near(distance, coef, acc):
+        name="sort",
+    )(pair_counts, in_hbm(pair_lists))
+
+    def near(group, coef, *acc):
         return pl.pallas_call(
-            functools.partial(near_kernel, distance),
+            functools.partial(near_kernel, group),
             out_shape=acc_shape,
-            in_specs=[SMEM, VMEM, VMEM, VMEM],
+            in_specs=[SMEM, VMEM, VMEM] + [VMEM] * len(acc),
             out_specs=VMEM,
-            input_output_aliases={3: 0},
+            input_output_aliases={3: 0} if acc else {},
             compiler_params=small,
             cost_estimate=cost(2),
-        )(table, ints, coef, acc)
-
-    acc = near(0, orbitals, acc)
+        )(table, ints, coef, *acc)
+
+    acc = near(0, orbitals)
     chunk, acc = lax.optimization_barrier((chunk, acc))
     chunks = [chunk] + [
         lax.ppermute(chunk, "aux", exchange_pairs(k, aux_size)) for k in range(1, aux_size)
@@ -230,11 +240,11 @@
     halves_shape = jax.ShapeDtypeStruct((width, aux_total * columns), jnp.bfloat16)
     far_scratch = [pltpu.VMEM((aux_size * depth, columns), jnp.bfloat16)]
     far_params = pltpu.CompilerParams(
-        vmem_limit_bytes=(6 << 20) + 2 * columns * depth * aux_size
+        vmem_limit_bytes=(10 << 20) + 2 * columns * depth * aux_size
     )
     whole_pairs = (2 * depth) % width == 0
     acc = pl.pallas_call(
-        functools.partial(far_kernel, (0, 1), (0, 1)),
+        functools.partial(far_kernel, (0, 1)),
         out_shape=acc_shape,
         in_specs=[SMEM] + [VMEM] * 4,
         out_specs=VMEM,
@@ -246,7 +256,7 @@
     )(table, ints, *chunks[:2], acc)
     needed = tuple(range(2 if whole_pairs else 0, aux_size))
     _, halves, *pieces = pl.pallas_call(
-        functools.partial(last_kernel, (2, aux_size - 1), needed, occ_size),
+        functools.partial(last_kernel, needed, occ_size),
         out_shape=[acc_shape, halves_shape] + [piece_shape] * (occ_size - 1),
         in_specs=[SMEM, VMEM] + [VMEM] * (aux_size + 1),
         out_specs=[VMEM] * (occ_size + 1),

time: 40.8 us -> 39.8 us (0.975)
  Pallas kernels: 14.8 us -> 12.8 us
  local copies, waits for them, and re-layouts: 0.19 us -> 1.02 us
    pallas_call x5, Pallas kernels: 13.1 us -> 11.2 us  [the longest x1 4.49 us: per_device(): pl.pallas_call(functools.partial(last_kernel, needed, occ_size), out_shap...]
    unnamed x14 -> x4, local copies, waits for them, and re-layouts: 0.19 us -> 1.02 us
    ppermute x3, waiting for transfers between devices: 2.28 us -> 2.71 us  [per_device(): lax.ppermute(chunk, 'aux', exchange_pairs(k, aux_size))]
  transfers between devices with their start and end apart: 10 -> 10, of which waited for: 7 -> 7; matrix products, arithmetic and copies ran while one was open for 0% -> 0% of each run, Pallas kernels for 24% -> 21%
where the time goes in v4:
time: 39.8 us; the launch traced here: 39.6 us
  starting transfers between devices  14.3 us (36%)
  Pallas kernels  12.8 us (32%)
  waiting for transfers between devices  9 us (23%)
  between operations  1.61 us (4%)
  local copies, waits for them, and re-layouts  1.02 us (3%)
  other arithmetic  0.89 us (2%)
    ppermute x3, starting transfers between devices, per_device(): lax.ppermute(chunk, 'aux', exchange_pairs(k, aux_size))  4.75 us
    pallas_call x1, Pallas kernels, per_device(): pl.pallas_call(functools.partial(last_kernel, needed, occ_size), out_shap...  4.49 us
    ppermute x3, starting transfers between devices, per_device(): lax.ppermute(sent, 'aux', exchange_pairs(k, aux_size))  3.68 us
    ppermute x3, waiting for transfers between devices, per_device(): lax.ppermute(sent, 'aux', exchange_pairs(k, aux_size))  3.55 us
    pallas_call x2, Pallas kernels, near(): pl.pallas_call(functools.partial(near_kernel, group), out_shape=acc_shape...  3.21 us
    ppermute x1, starting transfers between devices, per_device(): next_block = lax.ppermute(orbitals, 'blk', exchange_pairs(1, blk_size))  3.05 us
    ppermute x3, waiting for transfers between devices, per_device(): lax.ppermute(chunk, 'aux', exchange_pairs(k, aux_size))  2.71 us
    ppermute x1, starting transfers between devices, per_device(): parts.append(lax.ppermute(sent, ('aux', 'blk'), pairs))  2.65 us
  transfers between devices with their start and end apart: 10, of which 7 were waited for; matrix products, arithmetic and copies ran while one was open for 0% of the time, Pallas kernels for 21%

profile of v4, /device:TPU:0, one launch (start us, length us, event | category | flops | bytes accessed | tf_op | source)
XLA Modules:
  0.0 39.6 jit_solution(6814862179971953496)
XLA Ops:
  0.0 3.1 %collective-permute-start.4 = (bf16[512,256]{1,0:T(8,128)(2,1)}, bf16[512,256]{1,0:T(8,128)(2,1)S(1)}, u32[]{:S(2)}, u32[]{:S(2)}) collective-permute-start(bf16[512,256]{1,0:T(8,128)(2,1)} %coef_ref.1), channel_id=1, source_target_pairs={{0,2},{2,0},{4,6},{6,4},{1,3},{3,1},{5,7},{7,5},{8,10},{10,8},{12,... | collective-permute-start | bytes 786440 | tf_op jit(solution)/shard_map/ppermute | solution.py:201
  3.1 1.1 %head.1 = bf16[256,256]{1,0:T(8,128)(2,1)S(1)} custom-call(bf16[512,256]{1,0:T(8,128)(2,1)} %coef_ref.1), custom_call_target="tpu_custom_call" | custom-call | flops 23622320128 | bytes 92274688 | tf_op jit(solution)/shard_map/head/pallas_call | solution.py:190
  4.1 0.0 copy-start.1
  4.1 2.7 %collective-permute-start = (bf16[256,256]{1,0:T(8,128)(2,1)S(1)}, bf16[256,256]{1,0:T(8,128)(2,1)S(1)}, u32[]{:S(2)}, u32[]{:S(2)}) collective-permute-start(bf16[256,256]{1,0:T(8,128)(2,1)S(1)} %head.1), channel_id=1, source_target_pairs={{0,4},{2,6},{4,0},{6,2},{8,12},{10,14},{12,8},{14,10},{16,22},{18,... | collective-permute-start | bytes 393224 | tf_op jit(solution)/shard_map/ppermute | solution.py:200
  8.2 1.6 %sort.1.table = s32[28]{0:T(128)S(1)} custom-call(s32[1]{0:T(128)S(6)} %copy.11.counts, s32[1,11]{1,0:T(1,128)} %lists_hbm.1), custom_call_target="tpu_custom_call" | custom-call | flops 536870912 | bytes 2097152 | tf_op jit(solution)/shard_map/sort/pallas_call | solution.py:209
  9.9 0.8 %copy-done = bf16[4,1,11,512,512]{4,3,2,1,0:T(8,128)(2,1)S(1)} copy-done((bf16[4,1,11,512,512]{4,3,2,1,0:T(8,128)(2,1)S(1)}, bf16[4,1,11,512,512]{4,3,2,1,0:T(8,128)(2,1)}, u32[]{:S(2)}) %copy-start) | copy-done | bytes 23068696
  10.7 0.2 copy-done.1
  10.9 2.0 %shard_map.46.accs_0_ = f32[4,512,256]{2,1,0:T(8,128)S(1)} custom-call(s32[28]{0:T(128)S(1)} %sort.1.table, bf16[4,1,11,512,512]{4,3,2,1,0:T(8,128)(2,1)S(1)} %copy-done, bf16[512,256]{1,0:T(8,128)(2,1)S(1)} %copy-done.1), custom_call_target="tpu_custom_call" | custom-call | flops 1073741824 | bytes 4194304 | tf_op jit(solution)/shard_map/pallas_call | solution.py:221
  12.8 0.0 collective-permute-done.rest_0_
  12.8 1.6 %collective-permute-start.1 = (bf16[256,256]{1,0:T(8,128)(2,1)S(1)}, bf16[256,256]{1,0:T(8,128)(2,1)S(1)}, u32[]{:S(2)}, u32[]{:S(2)}) collective-permute-start(bf16[256,256]{1,0:T(8,128)(2,1)S(1)} %collective-permute-done.rest_0_), channel_id=1, source_target_pairs={{0,8},{8,0},{16,24},{24,16},{1,9},{9,1},{17,25},{25,17},{2,10},{10... | collective-permute-start | bytes 393224 | tf_op jit(solution)/shard_map/ppermute | solution.py:234
  14.4 3.2 %collective-permute-start.2 = (bf16[256,256]{1,0:T(8,128)(2,1)S(1)}, bf16[256,256]{1,0:T(8,128)(2,1)S(1)}, u32[]{:S(2)}, u32[]{:S(2)}) collective-permute-start(bf16[256,256]{1,0:T(8,128)(2,1)S(1)} %collective-permute-done.rest_0_), channel_id=1, source_target_pairs={{0,16},{8,24},{16,0},{24,8},{1,17},{9,25},{17,1},{25,9},{2,18},{10... | collective-permute-start | bytes 393224 | tf_op jit(solution)/shard_map/ppermute | solution.py:234
  17.6 0.0 collective-permute-start.3
  17.6 0.0 collective-permute-done.4.coef_ref
  17.6 1.3 %shard_map.47.rest_2_ = f32[4,512,256]{2,1,0:T(8,128)S(1)} custom-call(s32[28]{0:T(128)S(1)} %sort.1.table, bf16[4,1,11,512,512]{4,3,2,1,0:T(8,128)(2,1)S(1)} %copy-done, bf16[512,256]{1,0:T(8,128)(2,1)S(1)} %collective-permute-done.4.coef_ref, f32[4,512,256]{2,1,0:T(8,128)S(1)} %shard_map.46.accs_0_), custom_call_target="tpu_custom_call", output_to_operand_aliasing={{}: (3, {})} | custom-call | flops 1073741824 | bytes 4194304 | tf_op jit(solution)/shard_map/pallas_call | solution.py:221
  18.9 0.0 collective-permute-done.1.rest_1_
  18.9 1.9 %far.1.rest_4_ = f32[4,512,256]{2,1,0:T(8,128)S(1)} custom-call(s32[28]{0:T(128)S(1)} %sort.1.table, bf16[4,1,11,512,512]{4,3,2,1,0:T(8,128)(2,1)S(1)} %copy-done, bf16[256,256]{1,0:T(8,128)(2,1)S(1)} %collective-permute-done.rest_0_, bf16[256,256]{1,0:T(8,128)(2,1)S(1)} %collective-permute-done.1.rest_1_, ...), custom_call_target="tpu_custom_call", output_to_operand_aliasing={{}: (4, {})} | custom-call | flops 1610612736 | bytes 6291456 | tf_op jit(solution)/shard_map/far/pallas_call | solution.py:246
  20.7 1.3 %collective-permute-done.2.rest_2_ = bf16[256,256]{1,0:T(8,128)(2,1)S(1)} collective-permute-done((bf16[256,256]{1,0:T(8,128)(2,1)S(1)}, bf16[256,256]{1,0:T(8,128)(2,1)S(1)}, u32[]{:S(2)}, u32[]{:S(2)}) %collective-permute-start.2) | collective-permute-done | bytes 131104 | tf_op jit(solution)/shard_map/ppermute | solution.py:234
  22.0 1.4 %collective-permute-done.3.rest_3_ = bf16[256,256]{1,0:T(8,128)(2,1)S(1)} collective-permute-done((bf16[256,256]{1,0:T(8,128)(2,1)S(1)}, bf16[256,256]{1,0:T(8,128)(2,1)S(1)}, u32[]{:S(2)}, u32[]{:S(2)}) %collective-permute-start.3) | collective-permute-done | bytes 131104 | tf_op jit(solution)/shard_map/ppermute | solution.py:234
  23.4 4.5 %last.1 = (f32[4,512,256]{2,1,0:T(8,128)S(1)}, bf16[512,1024]{1,0:T(8,128)(2,1)S(1)}, f32[512,256]{1,0:T(8,128)S(1)}) custom-call(s32[28]{0:T(128)S(1)} %sort.1.table, bf16[4,1,11,512,512]{4,3,2,1,0:T(8,128)(2,1)S(1)} %copy-done, bf16[256,256]{1,0:T(8,128)(2,1)S(1)} %collective-permute-done.rest_0_, ...), custom_call_target="tpu_custom_call", output_to_operand_aliasing={{0}: (6, {})} | custom-call | flops 1610612736 | bytes 6291456 | tf_op jit(solution)/shard_map/last/pallas_call | solution.py:258
  27.9 0.1 collective-permute-start.5
  28.0 0.5 %kept.1.refs_0_ = f32[512,256]{1,0:T(8,128)S(1)} custom-call(bf16[512,1024]{1,0:T(8,128)(2,1)S(1)} %get-tuple-element.15.halves), custom_call_target="tpu_custom_call" | custom-call | flops 536870912 | bytes 2097152 | tf_op jit(solution)/shard_map/kept/pallas_call | solution.py:269
  28.5 1.4 %collective-permute-done.5.refs_1_ = f32[512,256]{1,0:T(8,128)S(1)} collective-permute-done((f32[512,256]{1,0:T(8,128)S(1)}, f32[512,256]{1,0:T(8,128)S(1)}, u32[]{:S(2)}, u32[]{:S(2)}) %collective-permute-start.5) | collective-permute-done | bytes 524320 | tf_op jit(solution)/shard_map/ppermute | solution.py:280
  29.9 0.1 split.1
  30.0 0.9 %collective-permute-start.6 = (f16[144,256]{1,0:T(8,128)(2,1)S(1)}, f16[144,256]{1,0:T(8,128)(2,1)S(1)}, u32[]{:S(2)}, u32[]{:S(2)}) collective-permute-start(f16[144,256]{1,0:T(8,128)(2,1)S(1)} %convert_element_type.18), channel_id=1, source_target_pairs={{0,8},{8,0},{16,24},{24,16},{1,9},{9,1},{17,25},{25,17},{2,10},{10... | collective-permute-start | bytes 221192 | tf_op jit(solution)/shard_map/ppermute | solution.py:295
  30.9 1.1 %collective-permute-start.7 = (f16[144,256]{1,0:T(8,128)(2,1)S(1)}, f16[144,256]{1,0:T(8,128)(2,1)S(1)}, u32[]{:S(2)}, u32[]{:S(2)}) collective-permute-start(f16[144,256]{1,0:T(8,128)(2,1)S(1)} %convert_element_type.20), channel_id=1, source_target_pairs={{0,16},{8,24},{16,0},{24,8},{1,17},{9,25},{17,1},{25,9},{2,18},{10... | collective-permute-start | bytes 221192 | tf_op jit(solution)/shard_map/ppermute | solution.py:295
  32.0 1.7 %collective-permute-start.8 = (f16[144,256]{1,0:T(8,128)(2,1)S(1)}, f16[144,256]{1,0:T(8,128)(2,1)S(1)}, u32[]{:S(2)}, u32[]{:S(2)}) collective-permute-start(f16[144,256]{1,0:T(8,128)(2,1)S(1)} %convert_element_type.22), channel_id=1, source_target_pairs={{0,24},{8,16},{16,8},{24,0},{1,25},{9,17},{17,9},{25,1},{2,26},{10... | collective-permute-start | bytes 221192 | tf_op jit(solution)/shard_map/ppermute | solution.py:295
  33.8 0.7 %collective-permute-done.6 = f16[144,256]{1,0:T(8,128)(2,1)S(1)} collective-permute-done((f16[144,256]{1,0:T(8,128)(2,1)S(1)}, f16[144,256]{1,0:T(8,128)(2,1)S(1)}, u32[]{:S(2)}, u32[]{:S(2)}) %collective-permute-start.6) | collective-permute-done | bytes 73760 | tf_op jit(solution)/shard_map/ppermute | solution.py:295
  34.5 1.6 %collective-permute-done.7 = f16[144,256]{1,0:T(8,128)(2,1)S(1)} collective-permute-done((f16[144,256]{1,0:T(8,128)(2,1)S(1)}, f16[144,256]{1,0:T(8,128)(2,1)S(1)}, u32[]{:S(2)}, u32[]{:S(2)}) %collective-permute-start.7) | collective-permute-done | bytes 73760 | tf_op jit(solution)/shard_map/ppermute | solution.py:295
  36.2 1.2 %collective-permute-done.8 = f16[144,256]{1,0:T(8,128)(2,1)S(1)} collective-permute-done((f16[144,256]{1,0:T(8,128)(2,1)S(1)}, f16[144,256]{1,0:T(8,128)(2,1)S(1)}, u32[]{:S(2)}, u32[]{:S(2)}) %collective-permute-start.8) | collective-permute-done | bytes 73760 | tf_op jit(solution)/shard_map/ppermute | solution.py:295
  37.4 0.1 collective-permute-start.9
  37.5 1.3 %collective-permute-done.9 = f32[128,256]{1,0:T(8,128)S(1)} collective-permute-done((f32[128,256]{1,0:T(8,128)S(1)}, f32[128,256]{1,0:T(8,128)S(1)}, u32[]{:S(2)}, u32[]{:S(2)}) %collective-permute-start.9) | collective-permute-done | bytes 131104 | tf_op jit(solution)/shard_map/ppermute | solution.py:298
  38.9 0.7 %maximum_bitcast_fusion = f32[1,128,512]{2,1,0:T(8,128)} fusion(f32[128,256]{1,0:T(8,128)S(1)} %get-tuple-element.22, f32[128,256]{1,0:T(8,128)S(1)} %get-tuple-element.21), kind=kLoop, calls=%fused_computation | loop fusion | flops 65536 | bytes 524288 | tf_op jit(solution)/shard_map/broadcast_in_dim | solution.py:306
  (12 shorter events, 0.2 us)
Async XLA Ops:
  0.0 17.6 %collective-permute-start.4 = (bf16[512,256]{1,0:T(8,128)(2,1)}, bf16[512,256]{1,0:T(8,128)(2,1)S(1)}, u32[]{:S(2)}, u32[]{:S(2)}) collective-permute-start(bf16[512,256]{1,0:T(8,128)(2,1)} %coef_ref.1), channel_id=1, source_target_pairs={{0,2},{2,0},{4,6},{6,4},{1,3},{3,1},{5,7},{7,5},{8,10},{10,8},{12,... | collective-permute-start | bytes 786440 | tf_op jit(solution)/shard_map/ppermute | solution.py:201
  3.1 7.6 %copy-start = (bf16[4,1,11,512,512]{4,3,2,1,0:T(8,128)(2,1)S(1)}, bf16[4,1,11,512,512]{4,3,2,1,0:T(8,128)(2,1)}, u32[]{:S(2)}) copy-start(bf16[4,1,11,512,512]{4,3,2,1,0:T(8,128)(2,1)} %ints_ref.7) | copy-start | bytes 69206016
  4.1 6.7 %copy-start.1 = (bf16[512,256]{1,0:T(8,128)(2,1)S(1)}, bf16[512,256]{1,0:T(8,128)(2,1)}, u32[]{:S(2)}) copy-start(bf16[512,256]{1,0:T(8,128)(2,1)} %coef_ref.1) | copy-start | bytes 786436
  4.1 8.7 %collective-permute-start = (bf16[256,256]{1,0:T(8,128)(2,1)S(1)}, bf16[256,256]{1,0:T(8,128)(2,1)S(1)}, u32[]{:S(2)}, u32[]{:S(2)}) collective-permute-start(bf16[256,256]{1,0:T(8,128)(2,1)S(1)} %head.1), channel_id=1, source_target_pairs={{0,4},{2,6},{4,0},{6,2},{8,12},{10,14},{12,8},{14,10},{16,22},{18,... | collective-permute-start | bytes 393224 | tf_op jit(solution)/shard_map/ppermute | solution.py:200
  12.8 6.0 %collective-permute-start.1 = (bf16[256,256]{1,0:T(8,128)(2,1)S(1)}, bf16[256,256]{1,0:T(8,128)(2,1)S(1)}, u32[]{:S(2)}, u32[]{:S(2)}) collective-permute-start(bf16[256,256]{1,0:T(8,128)(2,1)S(1)} %collective-permute-done.rest_0_), channel_id=1, source_target_pairs={{0,8},{8,0},{16,24},{24,16},{1,9},{9,1},{17,25},{25,17},{2,10},{10... | collective-permute-start | bytes 393224 | tf_op jit(solution)/shard_map/ppermute | solution.py:234
  14.4 7.6 %collective-permute-start.2 = (bf16[256,256]{1,0:T(8,128)(2,1)S(1)}, bf16[256,256]{1,0:T(8,128)(2,1)S(1)}, u32[]{:S(2)}, u32[]{:S(2)}) collective-permute-start(bf16[256,256]{1,0:T(8,128)(2,1)S(1)} %collective-permute-done.rest_0_), channel_id=1, source_target_pairs={{0,16},{8,24},{16,0},{24,8},{1,17},{9,25},{17,1},{25,9},{2,18},{10... | collective-permute-start | bytes 393224 | tf_op jit(solution)/shard_map/ppermute | solution.py:234
  17.6 5.9 %collective-permute-start.3 = (bf16[256,256]{1,0:T(8,128)(2,1)S(1)}, bf16[256,256]{1,0:T(8,128)(2,1)S(1)}, u32[]{:S(2)}, u32[]{:S(2)}) collective-permute-start(bf16[256,256]{1,0:T(8,128)(2,1)S(1)} %collective-permute-done.rest_0_), channel_id=1, source_target_pairs={{0,24},{8,16},{16,8},{24,0},{1,25},{9,17},{17,9},{25,1},{2,26},{10... | collective-permute-start | bytes 393224 | tf_op jit(solution)/shard_map/ppermute | solution.py:234
  27.9 2.0 %collective-permute-start.5 = (f32[512,256]{1,0:T(8,128)S(1)}, f32[512,256]{1,0:T(8,128)S(1)}, u32[]{:S(2)}, u32[]{:S(2)}) collective-permute-start(f32[512,256]{1,0:T(8,128)S(1)} %get-tuple-element.16), channel_id=1, source_target_pairs={{0,1},{1,0},{2,3},{3,2},{4,5},{5,4},{6,7},{7,6},{8,9},{9,8},{10,11... | collective-permute-start | bytes 1572872 | tf_op jit(solution)/shard_map/ppermute | solution.py:280
  30.0 4.4 %collective-permute-start.6 = (f16[144,256]{1,0:T(8,128)(2,1)S(1)}, f16[144,256]{1,0:T(8,128)(2,1)S(1)}, u32[]{:S(2)}, u32[]{:S(2)}) collective-permute-start(f16[144,256]{1,0:T(8,128)(2,1)S(1)} %convert_element_type.18), channel_id=1, source_target_pairs={{0,8},{8,0},{16,24},{24,16},{1,9},{9,1},{17,25},{25,17},{2,10},{10... | collective-permute-start | bytes 221192 | tf_op jit(solution)/shard_map/ppermute | solution.py:295
  30.9 5.2 %collective-permute-start.7 = (f16[144,256]{1,0:T(8,128)(2,1)S(1)}, f16[144,256]{1,0:T(8,128)(2,1)S(1)}, u32[]{:S(2)}, u32[]{:S(2)}) collective-permute-start(f16[144,256]{1,0:T(8,128)(2,1)S(1)} %convert_element_type.20), channel_id=1, source_target_pairs={{0,16},{8,24},{16,0},{24,8},{1,17},{9,25},{17,1},{25,9},{2,18},{10... | collective-permute-start | bytes 221192 | tf_op jit(solution)/shard_map/ppermute | solution.py:295
  32.0 5.3 %collective-permute-start.8 = (f16[144,256]{1,0:T(8,128)(2,1)S(1)}, f16[144,256]{1,0:T(8,128)(2,1)S(1)}, u32[]{:S(2)}, u32[]{:S(2)}) collective-permute-start(f16[144,256]{1,0:T(8,128)(2,1)S(1)} %convert_element_type.22), channel_id=1, source_target_pairs={{0,24},{8,16},{16,8},{24,0},{1,25},{9,17},{17,9},{25,1},{2,26},{10... | collective-permute-start | bytes 221192 | tf_op jit(solution)/shard_map/ppermute | solution.py:295
  37.4 1.4 %collective-permute-start.9 = (f32[128,256]{1,0:T(8,128)S(1)}, f32[128,256]{1,0:T(8,128)S(1)}, u32[]{:S(2)}, u32[]{:S(2)}) collective-permute-start(f32[128,256]{1,0:T(8,128)S(1)} %fusion.1), channel_id=1, source_target_pairs={{0,1},{1,0},{2,3},{3,2},{4,5},{5,4},{6,7},{7,6},{8,9},{9,8},{10,11... | collective-permute-start | bytes 393224 | tf_op jit(solution)/shard_map/ppermute | solution.py:298

commit v5 on v4

--- a/solution.py
+++ b/solution.py
@@ -61,21 +61,23 @@
     return (table[ends + group - 1] if group else 0), table[ends + group]
 
 
-def head_kernel(piece, t, coef_hbm, out_ref, sem):
+def head_kernel(piece, t, flips, coef_hbm, *rest):
+    *outs, sems = rest
     width = coef_hbm.shape[0]
     depth = (lax.axis_size("blk") - 2) * width // lax.axis_size("aux")
-    start = lax.rem(lax.axis_index("aux") * depth + t * piece, width)
-    rows = pl.ds(pl.multiple_of(start, piece), piece)
-    copy = pltpu.make_async_copy(coef_hbm.at[rows], out_ref, sem)
-    copy.start()
-    copy.wait()
-
-
-def sort_kernel(far_depth, width, counts, lists_hbm, table, lists, sem):
+    copies = []
+    for i, flip in enumerate(flips):
+        start = lax.rem((lax.axis_index("aux") ^ flip) * depth + t * piece, width)
+        rows = pl.ds(pl.multiple_of(start, piece), piece)
+        copies.append(pltpu.make_async_copy(coef_hbm.at[rows], outs[i], sems.at[i]))
+    for copy in copies:
+        copy.start()
+    for copy in copies:
+        copy.wait()
+
+
+def sort_kernel(far_depth, width, counts, lists, table):
     slot_total = lists.shape[1]
-    copy = pltpu.make_async_copy(lists_hbm, lists, sem)
-    copy.start()
-    copy.wait()
     me, my_aux = lax.axis_index("blk"), lax.axis_index("aux")
     live = counts[0]
     piece = math.gcd(far_depth, width)
@@ -179,27 +181,36 @@
 
     depth = (blk_size - 2) * width // aux_size
     piece = math.gcd(depth, width)
-    parts = []
-    for t in range(depth // piece):
-        starts = [a * depth + t * piece for a in range(aux_size)]
-        pairs = [
-            (a * blk_size + i, a * blk_size + (i ^ (2 + starts[a] // width)))
-            for a in range(aux_size)
-            for i in range(blk_size)
-        ]
-        sent = pl.pallas_call(
-            functools.partial(head_kernel, piece, t),
-            out_shape=jax.ShapeDtypeStruct((piece, columns), orbitals.dtype),
+
+    flips = (0, aux_size - 1)
+    to_send = [
+        pl.pallas_call(
+            functools.partial(head_kernel, piece, t, flips),
+            out_shape=[jax.ShapeDtypeStruct((piece, columns), orbitals.dtype)] * 2,
             in_specs=[HBM],
-            out_specs=VMEM,
-            scratch_shapes=[pltpu.SemaphoreType.DMA],
+            out_specs=[VMEM] * 2,
+            scratch_shapes=[pltpu.SemaphoreType.DMA((2,))],
             compiler_params=pltpu.CompilerParams(vmem_limit_bytes=1 << 20),
-            cost_estimate=cost(4 * slot_total),
+            cost_estimate=cost(16 * slot_total),
             name="head",
         )(in_hbm(orbitals))
-        parts.append(lax.ppermute(sent, ("aux", "blk"), pairs))
+        for t in range(depth // piece)
+    ]
+
+    def fetch_chunk(flip, rows):
+        parts = []
+        for t, sent in enumerate(rows):
+            starts = [(a ^ flip) * depth + t * piece for a in range(aux_size)]
+            pairs = [
+                (a * blk_size + i, a * blk_size + (i ^ (2 + starts[a] // width)))
+                for a in range(aux_size)
+                for i in range(blk_size)
+            ]
+            parts.append(lax.ppermute(sent, ("aux", "blk"), pairs))
+        return parts[0] if len(parts) == 1 else jnp.concatenate(parts, 0)
+
+    chunk = fetch_chunk(flips[0], [rows for rows, _ in to_send])
     next_block = lax.ppermute(orbitals, "blk", exchange_pairs(1, blk_size))
-    chunk = parts[0] if len(parts) == 1 else jnp.concatenate(parts, 0)
 
     acc_shape = jax.ShapeDtypeStruct((aux_total, width, columns), jnp.float32)
     table_shape = jax.ShapeDtypeStruct((2 * slot_total + 6,), jnp.int32)
@@ -209,13 +220,12 @@
     table = pl.pallas_call(
         functools.partial(sort_kernel, depth, width),
         out_shape=table_shape,
-        in_specs=[SMEM, HBM],
+        in_specs=[SMEM, SMEM],
         out_specs=SMEM,
-        scratch_shapes=[pltpu.SMEM(pair_lists.shape, jnp.int32), pltpu.SemaphoreType.DMA],
         compiler_params=pltpu.CompilerParams(vmem_limit_bytes=1 << 20),
         cost_estimate=cost(1),
         name="sort",
-    )(pair_counts, in_hbm(pair_lists))
+    )(pair_counts, pair_lists)
 
     def near(group, coef, *acc):
         return pl.pallas_call(
@@ -229,10 +239,12 @@
         )(table, ints, coef, *acc)
 
     acc = near(0, orbitals)
-    chunk, acc = lax.optimization_barrier((chunk, acc))
+    across = [rows for _, rows in to_send]
+    chunk, acc, across = lax.optimization_barrier((chunk, acc, across))
     chunks = [chunk] + [
-        lax.ppermute(chunk, "aux", exchange_pairs(k, aux_size)) for k in range(1, aux_size)
+        lax.ppermute(chunk, "aux", exchange_pairs(k, aux_size)) for k in range(1, aux_size - 1)
     ]
+    chunks.append(fetch_chunk(flips[1], across))
     acc = near(1, next_block, acc)
 
     share = width // occ_size

time: 39.8 us -> 40 us (level)
  starting transfers between devices: 14.3 us -> 15.7 us
  waiting for transfers between devices: 9 us -> 7.7 us
    ppermute x3 -> x2, waiting for transfers between devices: 2.71 us -> 0.01 us  [per_device(): lax.ppermute(chunk, 'aux', exchange_pairs(k, aux_size))]
    ppermute x1 -> x2, waiting for transfers between devices: 0.01 us -> 2.18 us  [fetch_chunk(): parts.append(lax.ppermute(sent, ('aux', 'blk'), pairs))]
    ppermute x1 -> x2, starting transfers between devices: 2.65 us -> 4.17 us  [fetch_chunk(): parts.append(lax.ppermute(sent, ('aux', 'blk'), pairs))]
    ppermute x3, waiting for transfers between devices: 3.55 us -> 2.77 us  [per_device(): lax.ppermute(sent, 'aux', exchange_pairs(k, aux_size))]
    unnamed x4 -> x6, local copies, waits for them, and re-layouts: 1.02 us -> 1.26 us
    ppermute x3 -> x2, starting transfers between devices: 4.75 us -> 4.68 us  [per_device(): lax.ppermute(chunk, 'aux', exchange_pairs(k, aux_size))]
  transfers between devices with their start and end apart: 10 -> 10, of which waited for: 7 -> 5; matrix products, arithmetic and copies ran while one was open for 0% -> 0% of each run, Pallas kernels for 21% -> 20%
where the time goes in v5:
time: 40 us; the launch traced here: 39.8 us
  starting transfers between devices  15.7 us (39%)
  Pallas kernels  12.6 us (32%)
  waiting for transfers between devices  7.7 us (19%)
  between operations  1.65 us (4%)
  local copies, waits for them, and re-layouts  1.26 us (3%)
  other arithmetic  0.89 us (2%)
    ppermute x2, starting transfers between devices, per_device(): lax.ppermute(chunk, 'aux', exchange_pairs(k, aux_size))  4.68 us
    pallas_call x1, Pallas kernels, per_device(): pl.pallas_call(functools.partial(last_kernel, needed, occ_size), out_shap...  4.49 us
    ppermute x2, starting transfers between devices, fetch_chunk(): parts.append(lax.ppermute(sent, ('aux', 'blk'), pairs))  4.17 us
    ppermute x3, starting transfers between devices, per_device(): lax.ppermute(sent, 'aux', exchange_pairs(k, aux_size))  3.67 us
    pallas_call x2, Pallas kernels, near(): pl.pallas_call(functools.partial(near_kernel, group), out_shape=acc_shape...  3.22 us
    ppermute x1, starting transfers between devices, per_device(): next_block = lax.ppermute(orbitals, 'blk', exchange_pairs(1, blk_size))  3.05 us
    ppermute x3, waiting for transfers between devices, per_device(): lax.ppermute(sent, 'aux', exchange_pairs(k, aux_size))  2.77 us
    ppermute x2, waiting for transfers between devices, fetch_chunk(): parts.append(lax.ppermute(sent, ('aux', 'blk'), pairs))  2.18 us
  transfers between devices with their start and end apart: 10, of which 5 were waited for; matrix products, arithmetic and copies ran while one was open for 0% of the time, Pallas kernels for 20%

profile of v5, /device:TPU:0, one launch (start us, length us, event | category | flops | bytes accessed | tf_op | source)
XLA Modules:
  0.0 39.8 jit_solution(7829432625679660787)
XLA Ops:
  0.0 3.1 %collective-permute-start.4 = (bf16[512,256]{1,0:T(8,128)(2,1)}, bf16[512,256]{1,0:T(8,128)(2,1)S(1)}, u32[]{:S(2)}, u32[]{:S(2)}) collective-permute-start(bf16[512,256]{1,0:T(8,128)(2,1)} %coef_ref.1), channel_id=1, source_target_pairs={{0,2},{2,0},{4,6},{6,4},{1,3},{3,1},{5,7},{7,5},{8,10},{10,8},{12,... | collective-permute-start | bytes 786440 | tf_op jit(solution)/shard_map/ppermute | solution.py:213
  3.1 1.1 %head.1 = (bf16[256,256]{1,0:T(8,128)(2,1)S(1)}, bf16[256,256]{1,0:T(8,128)(2,1)S(1)}) custom-call(bf16[512,256]{1,0:T(8,128)(2,1)} %coef_ref.1), custom_call_target="tpu_custom_call" | custom-call | flops 94489280512 | bytes 369098752 | tf_op jit(solution)/shard_map/head/pallas_call | solution.py:187
  4.2 0.0 copy-start.1
  4.2 2.7 %collective-permute-start = (bf16[256,256]{1,0:T(8,128)(2,1)S(1)}, bf16[256,256]{1,0:T(8,128)(2,1)S(1)}, u32[]{:S(2)}, u32[]{:S(2)}) collective-permute-start(bf16[256,256]{1,0:T(8,128)(2,1)S(1)} %get-tuple-element.16), channel_id=1, source_target_pairs={{0,4},{2,6},{4,0},{6,2},{8,12},{10,14},{12,8},{14,10},{16,22},{18,... | collective-permute-start | bytes 393224 | tf_op jit(solution)/shard_map/ppermute | solution.py:209
  8.3 1.3 %sort.1.table = s32[28]{0:T(128)S(1)} custom-call(s32[1]{0:T(128)S(6)} %copy.11.counts, s32[1,11]{1,0:T(1,128)S(1)} %copy-done.2), custom_call_target="tpu_custom_call" | custom-call | flops 536870912 | bytes 2097152 | tf_op jit(solution)/shard_map/sort/pallas_call | solution.py:220
  9.7 1.1 %copy-done = bf16[4,1,11,512,512]{4,3,2,1,0:T(8,128)(2,1)S(1)} copy-done((bf16[4,1,11,512,512]{4,3,2,1,0:T(8,128)(2,1)S(1)}, bf16[4,1,11,512,512]{4,3,2,1,0:T(8,128)(2,1)}, u32[]{:S(2)}) %copy-start) | copy-done | bytes 23068696
  10.8 0.2 copy-done.1
  10.9 2.0 %shard_map.46.accs_0_ = f32[4,512,256]{2,1,0:T(8,128)S(1)} custom-call(s32[28]{0:T(128)S(1)} %sort.1.table, bf16[4,1,11,512,512]{4,3,2,1,0:T(8,128)(2,1)S(1)} %copy-done, bf16[512,256]{1,0:T(8,128)(2,1)S(1)} %copy-done.1), custom_call_target="tpu_custom_call" | custom-call | flops 1073741824 | bytes 4194304 | tf_op jit(solution)/shard_map/pallas_call | solution.py:231
  12.9 0.0 collective-permute-done.rest_0_
  12.9 1.6 %collective-permute-start.1 = (bf16[256,256]{1,0:T(8,128)(2,1)S(1)}, bf16[256,256]{1,0:T(8,128)(2,1)S(1)}, u32[]{:S(2)}, u32[]{:S(2)}) collective-permute-start(bf16[256,256]{1,0:T(8,128)(2,1)S(1)} %collective-permute-done.rest_0_), channel_id=1, source_target_pairs={{0,8},{8,0},{16,24},{24,16},{1,9},{9,1},{17,25},{25,17},{2,10},{10... | collective-permute-start | bytes 393224 | tf_op jit(solution)/shard_map/ppermute | solution.py:245
  14.5 3.1 %collective-permute-start.2 = (bf16[256,256]{1,0:T(8,128)(2,1)S(1)}, bf16[256,256]{1,0:T(8,128)(2,1)S(1)}, u32[]{:S(2)}, u32[]{:S(2)}) collective-permute-start(bf16[256,256]{1,0:T(8,128)(2,1)S(1)} %collective-permute-done.rest_0_), channel_id=1, source_target_pairs={{0,16},{8,24},{16,0},{24,8},{1,17},{9,25},{17,1},{25,9},{2,18},{10... | collective-permute-start | bytes 393224 | tf_op jit(solution)/shard_map/ppermute | solution.py:245
  17.6 1.5 %collective-permute-start.3 = (bf16[256,256]{1,0:T(8,128)(2,1)S(1)}, bf16[256,256]{1,0:T(8,128)(2,1)S(1)}, u32[]{:S(2)}, u32[]{:S(2)}) collective-permute-start(bf16[256,256]{1,0:T(8,128)(2,1)S(1)} %get-tuple-element.19), channel_id=1, source_target_pairs={{0,6},{2,4},{4,2},{6,0},{8,14},{10,12},{12,10},{14,8},{16,20},{18,... | collective-permute-start | bytes 393224 | tf_op jit(solution)/shard_map/ppermute | solution.py:209
  19.1 0.0 collective-permute-done.4.coef_ref
  19.1 1.3 %shard_map.47.rest_2_ = f32[4,512,256]{2,1,0:T(8,128)S(1)} custom-call(s32[28]{0:T(128)S(1)} %sort.1.table, bf16[4,1,11,512,512]{4,3,2,1,0:T(8,128)(2,1)S(1)} %copy-done, bf16[512,256]{1,0:T(8,128)(2,1)S(1)} %collective-permute-done.4.coef_ref, f32[4,512,256]{2,1,0:T(8,128)S(1)} %shard_map.46.accs_0_), custom_call_target="tpu_custom_call", output_to_operand_aliasing={{}: (3, {})} | custom-call | flops 1073741824 | bytes 4194304 | tf_op jit(solution)/shard_map/pallas_call | solution.py:231
  20.4 0.0 collective-permute-done.1.rest_1_
  20.4 1.9 %far.1.rest_4_ = f32[4,512,256]{2,1,0:T(8,128)S(1)} custom-call(s32[28]{0:T(128)S(1)} %sort.1.table, bf16[4,1,11,512,512]{4,3,2,1,0:T(8,128)(2,1)S(1)} %copy-done, bf16[256,256]{1,0:T(8,128)(2,1)S(1)} %collective-permute-done.rest_0_, bf16[256,256]{1,0:T(8,128)(2,1)S(1)} %collective-permute-done.1.rest_1_, ...), custom_call_target="tpu_custom_call", output_to_operand_aliasing={{}: (4, {})} | custom-call | flops 1610612736 | bytes 6291456 | tf_op jit(solution)/shard_map/far/pallas_call | solution.py:258
  22.3 0.0 collective-permute-done.2.rest_2_
  22.3 2.2 %collective-permute-done.3.rest_3_ = bf16[256,256]{1,0:T(8,128)(2,1)S(1)} collective-permute-done((bf16[256,256]{1,0:T(8,128)(2,1)S(1)}, bf16[256,256]{1,0:T(8,128)(2,1)S(1)}, u32[]{:S(2)}, u32[]{:S(2)}) %collective-permute-start.3) | collective-permute-done | bytes 131104 | tf_op jit(solution)/shard_map/ppermute | solution.py:209
  24.4 4.5 %last.1 = (f32[4,512,256]{2,1,0:T(8,128)S(1)}, bf16[512,1024]{1,0:T(8,128)(2,1)S(1)}, f32[512,256]{1,0:T(8,128)S(1)}) custom-call(s32[28]{0:T(128)S(1)} %sort.1.table, bf16[4,1,11,512,512]{4,3,2,1,0:T(8,128)(2,1)S(1)} %copy-done, bf16[256,256]{1,0:T(8,128)(2,1)S(1)} %collective-permute-done.rest_0_, ...), custom_call_target="tpu_custom_call", output_to_operand_aliasing={{0}: (6, {})} | custom-call | flops 1610612736 | bytes 6291456 | tf_op jit(solution)/shard_map/last/pallas_call | solution.py:270
  28.9 0.1 collective-permute-start.5
  29.0 0.5 %kept.1.refs_0_ = f32[512,256]{1,0:T(8,128)S(1)} custom-call(bf16[512,1024]{1,0:T(8,128)(2,1)S(1)} %get-tuple-element.21.halves), custom_call_target="tpu_custom_call" | custom-call | flops 536870912 | bytes 2097152 | tf_op jit(solution)/shard_map/kept/pallas_call | solution.py:281
  29.5 1.4 %collective-permute-done.5.refs_1_ = f32[512,256]{1,0:T(8,128)S(1)} collective-permute-done((f32[512,256]{1,0:T(8,128)S(1)}, f32[512,256]{1,0:T(8,128)S(1)}, u32[]{:S(2)}, u32[]{:S(2)}) %collective-permute-start.5) | collective-permute-done | bytes 524320 | tf_op jit(solution)/shard_map/ppermute | solution.py:292
  30.9 0.1 split.1
  31.0 0.6 %collective-permute-start.6 = (f16[144,256]{1,0:T(8,128)(2,1)S(1)}, f16[144,256]{1,0:T(8,128)(2,1)S(1)}, u32[]{:S(2)}, u32[]{:S(2)}) collective-permute-start(f16[144,256]{1,0:T(8,128)(2,1)S(1)} %convert_element_type.18), channel_id=1, source_target_pairs={{0,8},{8,0},{16,24},{24,16},{1,9},{9,1},{17,25},{25,17},{2,10},{10... | collective-permute-start | bytes 221192 | tf_op jit(solution)/shard_map/ppermute | solution.py:307
  31.7 0.1 collective-permute-start.7
  31.8 3.0 %collective-permute-start.8 = (f16[144,256]{1,0:T(8,128)(2,1)S(1)}, f16[144,256]{1,0:T(8,128)(2,1)S(1)}, u32[]{:S(2)}, u32[]{:S(2)}) collective-permute-start(f16[144,256]{1,0:T(8,128)(2,1)S(1)} %convert_element_type.22), channel_id=1, source_target_pairs={{0,24},{8,16},{16,8},{24,0},{1,25},{9,17},{17,9},{25,1},{2,26},{10... | collective-permute-start | bytes 221192 | tf_op jit(solution)/shard_map/ppermute | solution.py:307
  34.8 0.7 %collective-permute-done.6 = f16[144,256]{1,0:T(8,128)(2,1)S(1)} collective-permute-done((f16[144,256]{1,0:T(8,128)(2,1)S(1)}, f16[144,256]{1,0:T(8,128)(2,1)S(1)}, u32[]{:S(2)}, u32[]{:S(2)}) %collective-permute-start.6) | collective-permute-done | bytes 73760 | tf_op jit(solution)/shard_map/ppermute | solution.py:307
  35.5 2.0 %collective-permute-done.7 = f16[144,256]{1,0:T(8,128)(2,1)S(1)} collective-permute-done((f16[144,256]{1,0:T(8,128)(2,1)S(1)}, f16[144,256]{1,0:T(8,128)(2,1)S(1)}, u32[]{:S(2)}, u32[]{:S(2)}) %collective-permute-start.7) | collective-permute-done | bytes 73760 | tf_op jit(solution)/shard_map/ppermute | solution.py:307
  37.6 0.0 collective-permute-done.8
  37.7 0.1 collective-permute-start.9
  37.8 1.3 %collective-permute-done.9 = f32[128,256]{1,0:T(8,128)S(1)} collective-permute-done((f32[128,256]{1,0:T(8,128)S(1)}, f32[128,256]{1,0:T(8,128)S(1)}, u32[]{:S(2)}, u32[]{:S(2)}) %collective-permute-start.9) | collective-permute-done | bytes 131104 | tf_op jit(solution)/shard_map/ppermute | solution.py:310
  39.1 0.7 %maximum_bitcast_fusion = f32[1,128,512]{2,1,0:T(8,128)} fusion(f32[128,256]{1,0:T(8,128)S(1)} %get-tuple-element.28, f32[128,256]{1,0:T(8,128)S(1)} %get-tuple-element.27), kind=kLoop, calls=%fused_computation | loop fusion | flops 65536 | bytes 524288 | tf_op jit(solution)/shard_map/broadcast_in_dim | solution.py:318
  (14 shorter events, 0.2 us)
Async XLA Ops:
  0.0 8.3 %copy-start.2 = (s32[1,11]{1,0:T(1,128)S(1)}, s32[1,11]{1,0:T(1,128)}, u32[]{:S(2)}) copy-start(s32[1,11]{1,0:T(1,128)} %lists.1) | copy-start | bytes 136
  0.0 19.1 %collective-permute-start.4 = (bf16[512,256]{1,0:T(8,128)(2,1)}, bf16[512,256]{1,0:T(8,128)(2,1)S(1)}, u32[]{:S(2)}, u32[]{:S(2)}) collective-permute-start(bf16[512,256]{1,0:T(8,128)(2,1)} %coef_ref.1), channel_id=1, source_target_pairs={{0,2},{2,0},{4,6},{6,4},{1,3},{3,1},{5,7},{7,5},{8,10},{10,8},{12,... | collective-permute-start | bytes 786440 | tf_op jit(solution)/shard_map/ppermute | solution.py:213
  3.1 7.7 %copy-start = (bf16[4,1,11,512,512]{4,3,2,1,0:T(8,128)(2,1)S(1)}, bf16[4,1,11,512,512]{4,3,2,1,0:T(8,128)(2,1)}, u32[]{:S(2)}) copy-start(bf16[4,1,11,512,512]{4,3,2,1,0:T(8,128)(2,1)} %ints_ref.7) | copy-start | bytes 69206016
  4.2 6.7 %copy-start.1 = (bf16[512,256]{1,0:T(8,128)(2,1)S(1)}, bf16[512,256]{1,0:T(8,128)(2,1)}, u32[]{:S(2)}) copy-start(bf16[512,256]{1,0:T(8,128)(2,1)} %coef_ref.1) | copy-start | bytes 786436
  4.2 8.7 %collective-permute-start = (bf16[256,256]{1,0:T(8,128)(2,1)S(1)}, bf16[256,256]{1,0:T(8,128)(2,1)S(1)}, u32[]{:S(2)}, u32[]{:S(2)}) collective-permute-start(bf16[256,256]{1,0:T(8,128)(2,1)S(1)} %get-tuple-element.16), channel_id=1, source_target_pairs={{0,4},{2,6},{4,0},{6,2},{8,12},{10,14},{12,8},{14,10},{16,22},{18,... | collective-permute-start | bytes 393224 | tf_op jit(solution)/shard_map/ppermute | solution.py:209
  12.9 7.5 %collective-permute-start.1 = (bf16[256,256]{1,0:T(8,128)(2,1)S(1)}, bf16[256,256]{1,0:T(8,128)(2,1)S(1)}, u32[]{:S(2)}, u32[]{:S(2)}) collective-permute-start(bf16[256,256]{1,0:T(8,128)(2,1)S(1)} %collective-permute-done.rest_0_), channel_id=1, source_target_pairs={{0,8},{8,0},{16,24},{24,16},{1,9},{9,1},{17,25},{25,17},{2,10},{10... | collective-permute-start | bytes 393224 | tf_op jit(solution)/shard_map/ppermute | solution.py:245
  14.5 7.8 %collective-permute-start.2 = (bf16[256,256]{1,0:T(8,128)(2,1)S(1)}, bf16[256,256]{1,0:T(8,128)(2,1)S(1)}, u32[]{:S(2)}, u32[]{:S(2)}) collective-permute-start(bf16[256,256]{1,0:T(8,128)(2,1)S(1)} %collective-permute-done.rest_0_), channel_id=1, source_target_pairs={{0,16},{8,24},{16,0},{24,8},{1,17},{9,25},{17,1},{25,9},{2,18},{10... | collective-permute-start | bytes 393224 | tf_op jit(solution)/shard_map/ppermute | solution.py:245
  17.6 6.9 %collective-permute-start.3 = (bf16[256,256]{1,0:T(8,128)(2,1)S(1)}, bf16[256,256]{1,0:T(8,128)(2,1)S(1)}, u32[]{:S(2)}, u32[]{:S(2)}) collective-permute-start(bf16[256,256]{1,0:T(8,128)(2,1)S(1)} %get-tuple-element.19), channel_id=1, source_target_pairs={{0,6},{2,4},{4,2},{6,0},{8,14},{10,12},{12,10},{14,8},{16,20},{18,... | collective-permute-start | bytes 393224 | tf_op jit(solution)/shard_map/ppermute | solution.py:209
  28.9 2.0 %collective-permute-start.5 = (f32[512,256]{1,0:T(8,128)S(1)}, f32[512,256]{1,0:T(8,128)S(1)}, u32[]{:S(2)}, u32[]{:S(2)}) collective-permute-start(f32[512,256]{1,0:T(8,128)S(1)} %get-tuple-element.22), channel_id=1, source_target_pairs={{0,1},{1,0},{2,3},{3,2},{4,5},{5,4},{6,7},{7,6},{8,9},{9,8},{10,11... | collective-permute-start | bytes 1572872 | tf_op jit(solution)/shard_map/ppermute | solution.py:292
  31.0 4.4 %collective-permute-start.6 = (f16[144,256]{1,0:T(8,128)(2,1)S(1)}, f16[144,256]{1,0:T(8,128)(2,1)S(1)}, u32[]{:S(2)}, u32[]{:S(2)}) collective-permute-start(f16[144,256]{1,0:T(8,128)(2,1)S(1)} %convert_element_type.18), channel_id=1, source_target_pairs={{0,8},{8,0},{16,24},{24,16},{1,9},{9,1},{17,25},{25,17},{2,10},{10... | collective-permute-start | bytes 221192 | tf_op jit(solution)/shard_map/ppermute | solution.py:307
  31.7 5.9 %collective-permute-start.7 = (f16[144,256]{1,0:T(8,128)(2,1)S(1)}, f16[144,256]{1,0:T(8,128)(2,1)S(1)}, u32[]{:S(2)}, u32[]{:S(2)}) collective-permute-start(f16[144,256]{1,0:T(8,128)(2,1)S(1)} %convert_element_type.20), channel_id=1, source_target_pairs={{0,16},{8,24},{16,0},{24,8},{1,17},{9,25},{17,1},{25,9},{2,18},{10... | collective-permute-start | bytes 221192 | tf_op jit(solution)/shard_map/ppermute | solution.py:307
  31.8 5.8 %collective-permute-start.8 = (f16[144,256]{1,0:T(8,128)(2,1)S(1)}, f16[144,256]{1,0:T(8,128)(2,1)S(1)}, u32[]{:S(2)}, u32[]{:S(2)}) collective-permute-start(f16[144,256]{1,0:T(8,128)(2,1)S(1)} %convert_element_type.22), channel_id=1, source_target_pairs={{0,24},{8,16},{16,8},{24,0},{1,25},{9,17},{17,9},{25,1},{2,26},{10... | collective-permute-start | bytes 221192 | tf_op jit(solution)/shard_map/ppermute | solution.py:307
  37.7 1.4 %collective-permute-start.9 = (f32[128,256]{1,0:T(8,128)S(1)}, f32[128,256]{1,0:T(8,128)S(1)}, u32[]{:S(2)}, u32[]{:S(2)}) collective-permute-start(f32[128,256]{1,0:T(8,128)S(1)} %fusion.1), channel_id=1, source_target_pairs={{0,1},{1,0},{2,3},{3,2},{4,5},{5,4},{6,7},{7,6},{8,9},{9,8},{10,11... | collective-permute-start | bytes 393224 | tf_op jit(solution)/shard_map/ppermute | solution.py:310
